TPU v7x, 32 devices: a whole 2x2x4 slice. The times are simulated.
32 devices in a mesh: occ: 8 (over z, y), virt: 4 (over x, core).
Axes of the slice: x: 2, y: 2, z: 4, core: 2. Of those that a mesh axis runs over, the one named last changes fastest.
Arguments:
- factors: bfloat16 [768, 98304], P('virt', 'occ'), may hold values from -1 to 1
- occ_energy: float32 [64], replicated, may hold values from -2 to -0.5
- virt_energy: float32 [768], replicated, may hold values from 0.2 to 3
- pair_table: int32 [16, 2], P('occ'), may hold values from 0 to 63, as said below
- pair_count: int32 [8], P('occ'), may hold values from 0 to 2, as said below
Outputs:
- gamma: float32 [768, 98304], P('virt', 'occ')
Inputs may be any that keep to these rules, and one draw needn't show every extreme that they name: `pair_table`: each row holds two different orbitals. `pair_count`: the counts sum to exactly 8, and some host has exactly 2.
All inputs are finite; a program needn't handle non-finite values.
Results may differ from a plain program's by a relative error of at most 0.0029.
Values may be sent and summed in bfloat16 or wider, within the bound.
No kernel may reach another device: no remote copies, remote signals or barrier semaphores. Data moves between devices by JAX's collectives and lax.ppermute only.
A program may use at most 128 MiB of HBM per device.

v0:
```python
import jax
import jax.numpy as jnp
from jax import lax
from jax.sharding import PartitionSpec as P


def body(factors, occ_energy, virt_energy, pair_table, pair_count):
    tables, counts = (
        lax.all_gather(pair_table, "occ", axis=0, tiled=True),
        lax.all_gather(pair_count, "occ", axis=0, tiled=True),
    )
    hosts_total = lax.axis_size("occ")
    per_host = pair_table.shape[0]
    entries = jnp.arange(hosts_total * per_host, dtype=jnp.int32)
    active = entries % per_host < jnp.repeat(counts, per_host)
    live_total = per_host * hosts_total // 2
    slot_count = -(-live_total // hosts_total)
    ranking = jnp.cumsum(active.astype(jnp.int32)) - 1
    targets = jnp.arange(hosts_total * slot_count, dtype=jnp.int32)
    select = (active[None, :] & (ranking[None, :] == targets[:, None])).astype(jnp.int32)
    plan = jnp.sum(select[:, :, None] * tables[None, :, :], axis=1).reshape(
        hosts_total, slot_count, 2
    )
    enabled = jnp.max(select, axis=1).reshape(hosts_total, slot_count)
    column = lax.axis_index("virt")
    myself = lax.axis_index("occ")
    orbital_count = occ_energy.shape[0]
    slab_width = factors.shape[0]
    aux_local = factors.shape[1] // orbital_count
    slab_energy = lax.dynamic_slice_in_dim(virt_energy, column * slab_width, slab_width)
    source = lax.all_gather(factors, "virt", axis=0, tiled=True)
    source_cube = source.reshape(source.shape[0], aux_local, orbital_count)

    def one_slot(position, accumulated):
        orbitals = lax.dynamic_index_in_dim(plan, position, 1, keepdims=False)
        flags = lax.dynamic_index_in_dim(enabled, position, 1, keepdims=False)
        targets_flat = orbitals.T.reshape(-1)
        picked = jnp.take(source_cube, targets_flat, axis=2)
        outgoing = picked.reshape(source.shape[0], aux_local, 2, hosts_total)
        both = lax.all_to_all(outgoing, "occ", split_axis=3, concat_axis=1, tiled=True)
        left = both[:, :, 0, 0]
        right = both[:, :, 1, 0]
        mine = lax.dynamic_index_in_dim(orbitals, myself, 0, keepdims=False)
        live_here = lax.dynamic_index_in_dim(flags, myself, 0, keepdims=False).astype(jnp.float32)
        left_slab = lax.dynamic_slice_in_dim(left, column * slab_width, slab_width, 0)
        right_slab = lax.dynamic_slice_in_dim(right, column * slab_width, slab_width, 0)
        couple_rows = lax.dot_general(
            left_slab, right, (((1,), (1,)), ((), ())), preferred_element_type=jnp.float32
        )
        couple_cols = lax.dot_general(
            left, right_slab, (((1,), (1,)), ((), ())), preferred_element_type=jnp.float32
        )
        energy_sum = jnp.take(occ_energy, mine[0]) + jnp.take(occ_energy, mine[1])
        ampl_rows = couple_rows / (energy_sum - slab_energy[:, None] - virt_energy[None, :])
        ampl_cols = couple_cols / (energy_sum - virt_energy[:, None] - slab_energy[None, :])
        mixed_rows = ((2.0 * ampl_rows - ampl_cols.T) * live_here).astype(jnp.bfloat16)
        mixed_cols = ((2.0 * ampl_cols - ampl_rows.T) * live_here).astype(jnp.bfloat16)
        toward_first = jnp.dot(mixed_rows, right, preferred_element_type=jnp.float32)
        toward_second = lax.dot_general(
            mixed_cols, left, (((0,), (0,)), ((), ())), preferred_element_type=jnp.float32
        )
        packed = jnp.stack(
            [toward_first.astype(jnp.bfloat16), toward_second.astype(jnp.bfloat16)], axis=2
        )
        packed = packed.reshape(slab_width, hosts_total, aux_local, 2, 1)
        returned = lax.all_to_all(packed, "occ", split_axis=1, concat_axis=4, tiled=True)
        onehot = (
            targets_flat[:, None] == jnp.arange(orbital_count, dtype=jnp.int32)[None, :]
        ).astype(jnp.bfloat16)
        added = jnp.dot(
            returned.reshape(slab_width * aux_local, 2 * hosts_total),
            onehot,
            preferred_element_type=jnp.float32,
        )
        return accumulated + added.reshape(accumulated.shape)

    start = jnp.zeros(factors.shape, jnp.float32)
    return lax.fori_loop(0, slot_count, one_slot, start)


def solution(mesh):
    in_specs = (P("virt", "occ"), P(), P(), P("occ", None), P("occ"))
    out_specs = P("virt", "occ")
    return jax.shard_map(body, mesh=mesh, in_specs=in_specs, out_specs=out_specs, check_vma=False)
```

profile of v0, /device:TPU:8, one launch (start us, length us, event | category | flops | bytes accessed | tf_op | source)
XLA Modules:
  0.0 391.9 jit_solution(17097592554794598104)
XLA Ops:
  6.5 0.7 all-gather.3.cloned.1.call-update
  7.9 0.6 dynamic-slice.11
  8.5 0.8 dynamic-update-slice.2
  9.3 10.5 %all-reduce = s32[8]{0:T(128)S(1)} all-reduce(s32[8]{0:T(128)S(1)} %dynamic-update-slice.2), channel_id=1, replica_groups=mesh['occ'=8,'virt'=4] {'occ'}, use_global_device_ids=true, to_apply=%add | all-reduce | flops 8 | bytes 64
  20.0 16.1 %all-gather = s32[8,2,2]{2,1,0:T(2,128)S(1)} all-gather(s32[1,2,2]{2,1,0:T(2,128)S(1)} %bitcast.81), channel_id=1, replica_groups=mesh['occ'=8,'virt'=4] {'occ'}, dimensions={0}, use_global_device_ids=true | all-gather | bytes 144 | tf_op jit(solution)/shard_map/all_gather | solution.py:9
  36.7 93.4 %all-gather.3.cloned.1.call-done = bf16[768,12288]{1,0:T(8,128)(2,1)} async-done(((bf16[192,12288]{1,0:T(8,128)(2,1)}), bf16[768,12288]{1,0:T(8,128)(2,1)}) %all-gather.3.cloned.1.call-update) | async-done | bytes 18874384 | tf_op jit(solution)/shard_map/all_gather | solution.py:31
  130.1 24.6 %copy.41 = bf16[768,12288]{0,1:T(8,128)(2,1)} copy(bf16[768,12288]{1,0:T(8,128)(2,1)} %all-gather.3.cloned.1.call-done) | data formatting | bytes 37748736 | tf_op jit(solution)/shard_map/all_gather | solution.py:31
  154.7 19.9 %copy.42 = bf16[768,192,64]{0,1,2:T(8,128)(2,1)} copy(bf16[768,192,64]{0,2,1:T(8,128)(2,1)} %bitcast.71) | data formatting | bytes 37748736 | tf_op jit(solution)/shard_map/reshape | solution.py:32
  174.6 9.4 %gather_fusion = bf16[16,768,192]{1,2,0:T(8,128)(2,1)} fusion(bf16[768,192,64]{0,1,2:T(8,128)(2,1)} %copy.42, s32[1024]{0:T(1024)S(1)} %pad_clamp_fusion), kind=kCustom, calls=%fused_computation | custom fusion | bytes 9437248 | tf_op jit(solution)/shard_map/while/body/eval_jaxpr/jit(_take)/gather | solution.py:38
  184.0 7.3 %bitcast_select_fusion = bf16[768,192,2,8]{0,3,2,1:T(8,128)(2,1)} fusion(bf16[768,192,16]{0,1,2:T(8,128)(2,1)} %bitcast.70, pred[2,8]{1,0:T(4,128)(4,1)S(1)} %compare_and_fusion), kind=kLoop, calls=%fused_computation.1 | loop fusion | flops 2359296 | bytes 9437200 | tf_op jit(solution)/shard_map/while/body/eval_jaxpr/jit(_take)/select_n | solution.py:38
  191.3 8.2 %copy.44 = bf16[768,192,2,8]{0,2,1,3:T(2,128)(2,1)} copy(bf16[768,192,2,8]{0,3,2,1:T(8,128)(2,1)} %bitcast_select_fusion) | data formatting | bytes 9437184 | tf_op jit(solution)/shard_map/while/body/eval_jaxpr/jit(_take)/select_n | solution.py:38
  199.4 6.2 %all-to-all-start = ((bf16[768,192,2,8]{0,2,1,3:T(2,128)(2,1)}), bf16[768,192,2,8]{0,2,1,3:T(2,128)(2,1)}, u32[]{:S(2)}, u32[]{:S(2)}) async-start(bf16[768,192,2,8]{0,2,1,3:T(2,128)(2,1)} %copy.44), calls=%async_computation | async-start | bytes 9437184 | tf_op jit(solution)/shard_map/while/body/eval_jaxpr/all_to_all | solution.py:40
  205.7 0.6 fusion.46
  210.3 0.6 dynamic_slice.37
  211.7 0.6 fusion.47
  213.7 94.3 %all-to-all-done = bf16[768,192,2,8]{0,2,1,3:T(2,128)(2,1)} async-done(((bf16[768,192,2,8]{0,2,1,3:T(2,128)(2,1)}), bf16[768,192,2,8]{0,2,1,3:T(2,128)(2,1)}, u32[]{:S(2)}, u32[]{:S(2)}) %all-to-all-start) | async-done | bytes 4718624 | tf_op jit(solution)/shard_map/while/body/eval_jaxpr/all_to_all | solution.py:40
  308.0 3.2 copy.45
  311.2 0.3 fusion.45
  311.5 0.9 fusion.4
  312.4 1.0 fusion.1
  313.4 1.1 convolution_convert_fusion
  314.5 1.1 convolution_convert_fusion.1
  315.6 0.6 stack.13
  316.2 0.2 copy.51
  316.3 0.6 stack.12
  316.9 0.2 copy.50
  317.1 1.4 pad_maximum_fusion
  318.5 6.2 %all-to-all-start.1 = ((bf16[192,8,192,2,1]{2,0,3,4,1:T(8,128)(2,1)}), bf16[192,8,192,2,1]{2,0,3,4,1:T(8,128)(2,1)S(1)}, u32[]{:S(2)}, u32[]{:S(2)}) async-start(bf16[192,8,192,2,1]{2,0,3,4,1:T(8,128)(2,1)} %pad_maximum_fusion), calls=%async_computation.1 | async-start | bytes 3145728 | tf_op jit(solution)/shard_map/while/body/eval_jaxpr/all_to_all | solution.py:66
  324.8 34.6 %all-to-all-done.1 = bf16[192,8,192,2,1]{2,0,3,4,1:T(8,128)(2,1)S(1)} async-done(((bf16[192,8,192,2,1]{2,0,3,4,1:T(8,128)(2,1)}), bf16[192,8,192,2,1]{2,0,3,4,1:T(8,128)(2,1)S(1)}, u32[]{:S(2)}, u32[]{:S(2)}) %all-to-all-start.1) | async-done | bytes 1179680 | tf_op jit(solution)/shard_map/while/body/eval_jaxpr/all_to_all | solution.py:66
  359.6 1.7 reshape.205
  361.3 8.0 %fusion.30 = f32[36864,64]{1,0:T(8,128)} fusion(bf16[36864,16]{0,1:T(8,128)(2,1)S(1)} %reshape.205, s32[16]{0:T(128)S(1)} %reshape.206), kind=kOutput, calls=%fused_computation.38 | convolution fusion | flops 75498496 | bytes 10616896 | tf_op jit(solution)/shard_map/while/body/eval_jaxpr/dot_general | solution.py:70
  369.3 15.8 %reshape.207 = f32[192,12288]{1,0:T(8,128)} reshape(f32[36864,64]{1,0:T(8,128)} %fusion.30) | data formatting | bytes 18874368 | tf_op jit(solution)/shard_map/while/body/eval_jaxpr/reshape | solution.py:75
  (31 shorter events, 1.3 us)
Async XLA Ops:
  6.5 1.4 copy-start.3
  6.5 13.5 %copy-start.2 = (s32[2,2]{1,0:T(2,128)S(1)}, s32[2,2]{1,0:T(2,128)}, u32[]{:S(2)}) copy-start(s32[2,2]{1,0:T(2,128)} %param.8) | copy-start | bytes 52
  6.5 123.5 %all-gather.3.cloned.1.call-start = ((), (), s32[]{:S(2)}) async-start(), calls=%async_computation.2 | async-start | bytes 23592960 | tf_op jit(solution)/shard_map/all_gather | solution.py:31
  199.4 12.2 %copy-start.1 = (f32[64]{0:T(128)S(1)}, f32[64]{0:T(128)}, u32[]{:S(2)}) copy-start(f32[64]{0:T(128)} %param.6) | copy-start | bytes 772
  199.4 14.1 %copy-start = (f32[768]{0:T(1024)S(1)}, f32[768]{0:T(1024)}, u32[]{:S(2)}) copy-start(f32[768]{0:T(1024)} %param.7) | copy-start | bytes 9220
  199.4 108.6 %all-to-all-start = ((bf16[768,192,2,8]{0,2,1,3:T(2,128)(2,1)}), bf16[768,192,2,8]{0,2,1,3:T(2,128)(2,1)}, u32[]{:S(2)}, u32[]{:S(2)}) async-start(bf16[768,192,2,8]{0,2,1,3:T(2,128)(2,1)} %copy.44), calls=%async_computation | async-start | bytes 9437184 | tf_op jit(solution)/shard_map/while/body/eval_jaxpr/all_to_all | solution.py:40
  318.5 40.9 %all-to-all-start.1 = ((bf16[192,8,192,2,1]{2,0,3,4,1:T(8,128)(2,1)}), bf16[192,8,192,2,1]{2,0,3,4,1:T(8,128)(2,1)S(1)}, u32[]{:S(2)}, u32[]{:S(2)}) async-start(bf16[192,8,192,2,1]{2,0,3,4,1:T(8,128)(2,1)} %pad_maximum_fusion), calls=%async_computation.1 | async-start | bytes 3145728 | tf_op jit(solution)/shard_map/while/body/eval_jaxpr/all_to_all | solution.py:66
Sparse Core Ops, SparseCore 0:
  8.9 121.1 all-gather.2
where the time goes:
time: 397 us; the launch traced here: 392 us
  waiting for transfers between devices  223 us (56%)
  local copies, waits for them, and re-layouts  88.5 us (22%)
  blocking collectives  26.6 us (7%)
  between operations  20.1 us (5%)
  starting transfers between devices  12.4 us (3%)
  matrix products  12 us (3%)
  other arithmetic  9.26 us (2%)
    all_to_all x1, waiting for transfers between devices, one_slot(): lax.all_to_all(outgoing, 'occ', split_axis=3, concat_axis=1, tiled=True)  94.3 us
    all_gather x1, waiting for transfers between devices, body(): source = lax.all_gather(factors, 'virt', axis=0, tiled=True)  93.4 us
    all_to_all x1, waiting for transfers between devices, one_slot(): lax.all_to_all(packed, 'occ', split_axis=1, concat_axis=4, tiled=True)  34.6 us
    all_gather x1, local copies, waits for them, and re-layouts, body(): source = lax.all_gather(factors, 'virt', axis=0, tiled=True)  24.6 us
    reshape x1, local copies, waits for them, and re-layouts, body(): source_cube = source.reshape(source.shape[0], aux_local, orbital_count)  19.9 us
    all_gather x1, blocking collectives, body(): lax.all_gather(pair_table, 'occ', axis=0, tiled=True)  16.1 us
    reshape x1, local copies, waits for them, and re-layouts, one_slot(): return accumulated + added.reshape(accumulated.shape)  15.8 us
    unnamed x1, blocking collectives  10.5 us
  transfers between devices with their start and end apart: 3, of which 3 were waited for; matrix products, arithmetic and copies ran while one was open for 1% of the time, Pallas kernels for 0%

commit v1 on v0

v1 whole, which is shorter than its diff:
```python
import functools

import jax
import jax.numpy as jnp
from jax import lax
from jax.experimental import pallas as pl
from jax.experimental.pallas import tpu as pltpu
from jax.sharding import PartitionSpec as P

LANES = 128
STRIP = 16


def read_plan(tab_ref, me, hosts, per_host, first_ref, second_ref):
    for t in range(hosts):
        first_ref[t] = jnp.int32(-1)
        second_ref[t] = jnp.int32(-1)
    rank = jnp.int32(0)
    for h in range(hosts):
        slot = h ^ me
        count = tab_ref[slot, 2 * per_host]
        for r in range(per_host):
            live = (r < count) & (rank < hosts)

            @pl.when(live)
            def _(rank=rank, r=r, slot=slot):
                first_ref[rank] = tab_ref[slot, 2 * r]
                second_ref[rank] = tab_ref[slot, 2 * r + 1]

            rank = rank + live.astype(jnp.int32)


def pick_matrix(first_ref, second_ref, me, hosts, orbitals, sel_ref):
    width = STRIP * orbitals
    lane = lax.broadcasted_iota(jnp.int32, (STRIP, width), 1)
    row = lax.broadcasted_iota(jnp.int32, (STRIP, width), 0)
    here = lane - row * orbitals
    for s in range(hosts):
        for which, ref in enumerate((first_ref, second_ref)):
            orbital = ref[me ^ s]
            hit = (here == orbital) & (orbital >= 0)
            base = (which * hosts + s) * STRIP
            sel_ref[base:base + STRIP, :] = jnp.where(hit, 1.0, 0.0).astype(jnp.bfloat16)


def select_kernel(hosts, per_host, orbitals, strips, tab_ref, me_ref, x_ref, *rest):
    outs, (sel_ref, first_ref, second_ref) = rest[:hosts], rest[hosts:]
    me = me_ref[0]

    @pl.when(pl.program_id(0) == 0)
    def _():
        read_plan(tab_ref, me, hosts, per_host, first_ref, second_ref)
        pick_matrix(first_ref, second_ref, me, hosts, orbitals, sel_ref)

    width = STRIP * orbitals
    slab = x_ref.shape[0]
    for k in range(strips):
        picked = lax.dot_general(
            sel_ref[...], x_ref[:, k * width:(k + 1) * width], (((1,), (1,)), ((), ())),
            preferred_element_type=jnp.float32,
        ).astype(jnp.bfloat16)
        for s in range(hosts):
            left = picked[s * STRIP:(s + 1) * STRIP]
            right = picked[(hosts + s) * STRIP:(hosts + s + 1) * STRIP]
            outs[s][k * STRIP:(k + 1) * STRIP, :] = jnp.concatenate([left, right], axis=1)


def scatter_kernel(hosts, per_host, orbitals, strips, tab_ref, me_ref, *rest):
    ins, (out_ref, sel_ref, first_ref, second_ref) = rest[:hosts], rest[hosts:]
    me = me_ref[0]

    @pl.when(pl.program_id(0) == 0)
    def _():
        read_plan(tab_ref, me, hosts, per_host, first_ref, second_ref)
        pick_matrix(first_ref, second_ref, me, hosts, orbitals, sel_ref)

    width = STRIP * orbitals
    slab = out_ref.shape[0]
    for k in range(strips):
        rows = [ins[s][k * STRIP:(k + 1) * STRIP, :] for s in range(hosts)]
        stacked = jnp.concatenate([r[:, :slab] for r in rows] + [r[:, slab:] for r in rows], axis=0)
        out_ref[:, k * width:(k + 1) * width] = lax.dot_general(
            stacked, sel_ref[...], (((0,), (0,)), ((), ())), preferred_element_type=jnp.float32
        )


def pair_kernel(hosts, per_host, groups, step, tab_ref, me_ref, occ_ref, col_ref, row_ref, *rest):
    parts = rest[:groups]
    outs = rest[groups:groups + hosts]
    lall, rall, first_ref, second_ref = rest[groups + hosts:]
    me = me_ref[0]
    read_plan(tab_ref, me, hosts, per_host, first_ref, second_ref)
    i, j = first_ref[me], second_ref[me]
    live = jnp.where(i >= 0, 1.0, 0.0)
    energy = occ_ref[jnp.maximum(i, 0)] + occ_ref[jnp.maximum(j, 0)]
    slab = col_ref.shape[0]
    total, _ = lall.shape
    full = groups * slab

    def gather(c, carry):
        rows = pl.ds(pl.multiple_of(c * step, step), step)
        blocks = [parts[g][rows, :] for g in range(groups)]
        lall[rows, :] = jnp.concatenate([b[:, :slab] for b in blocks], axis=1)
        rall[rows, :] = jnp.concatenate([b[:, slab:] for b in blocks], axis=1)
        return carry

    lax.fori_loop(0, total // step, gather, 0)

    def couple(c, carry):
        one, two = carry
        rows = pl.ds(pl.multiple_of(c * step, step), step)
        dims = (((0,), (0,)), ((), ()))
        one = one + lax.dot_general(lall[rows, :slab], rall[rows, :], dims, preferred_element_type=jnp.float32)
        two = two + lax.dot_general(rall[rows, :slab], lall[rows, :], dims, preferred_element_type=jnp.float32)
        return one, two

    zero = jnp.zeros((slab, full), jnp.float32)
    one, two = lax.fori_loop(0, total // step, couple, (zero, zero))
    den = energy - col_ref[...] - row_ref[...]
    mixed_rows = (((2.0 * one - two) / den) * live).astype(jnp.bfloat16)
    mixed_cols = (((2.0 * two - one) / den) * live).astype(jnp.bfloat16)
    aux = total // hosts
    dims = (((1,), (1,)), ((), ()))
    for s in range(hosts):
        rows = slice(s * aux, (s + 1) * aux)
        toward_first = lax.dot_general(rall[rows, :], mixed_rows, dims, preferred_element_type=jnp.float32)
        toward_second = lax.dot_general(lall[rows, :], mixed_cols, dims, preferred_element_type=jnp.float32)
        outs[s][...] = jnp.concatenate(
            [toward_first.astype(jnp.bfloat16), toward_second.astype(jnp.bfloat16)], axis=1
        )


def fast_body(hosts, columns, factors, occ_energy, virt_energy, pair_table, pair_count):
    slab, local = factors.shape
    orbitals = occ_energy.shape[0]
    aux = local // orbitals
    per_host = pair_table.shape[0]
    me = lax.axis_index("occ").astype(jnp.int32)
    column = lax.axis_index("virt").astype(jnp.int32)
    vmem, smem = pltpu.VMEM, pltpu.SMEM

    table = jnp.concatenate([pair_table.reshape(1, -1), pair_count.reshape(1, 1)], axis=1)
    shift = 1
    while shift < hosts:
        other = lax.ppermute(table, "occ", [(d, d ^ shift) for d in range(hosts)])
        table = jnp.concatenate([table, other], axis=0)
        shift *= 2
    here = me.reshape(1)

    strips = 2 if aux % (2 * STRIP) == 0 else 1
    block = strips * STRIP
    width = block * orbitals
    steps = aux // block
    plan_scratch = [pltpu.SMEM((hosts,), jnp.int32), pltpu.SMEM((hosts,), jnp.int32)]
    sel_scratch = pltpu.VMEM((2 * hosts * STRIP, STRIP * orbitals), jnp.bfloat16)
    in_smem = pl.BlockSpec(memory_space=smem)
    in_vmem = pl.BlockSpec(memory_space=vmem)

    sent = pl.pallas_call(
        functools.partial(select_kernel, hosts, per_host, orbitals, strips),
        grid=(steps,),
        out_shape=[jax.ShapeDtypeStruct((aux, 2 * slab), jnp.bfloat16)] * hosts,
        in_specs=[in_smem, in_smem, pl.BlockSpec((slab, width), lambda g: (0, g))],
        out_specs=[pl.BlockSpec((block, 2 * slab), lambda g: (g, 0))] * hosts,
        scratch_shapes=[sel_scratch] + plan_scratch,
        name="select",
    )(table, here, factors)

    def exchange(pieces):
        got = {0: pieces[0]}
        for s in sorted(range(1, hosts), reverse=True):
            got[s] = lax.ppermute(pieces[s], "occ", [(d, d ^ s) for d in range(hosts)])
        return [got[s] for s in range(hosts)]

    arrived = exchange(sent)
    mine = jnp.concatenate(arrived, axis=0)
    parts = [mine]
    shift = columns // 2
    order = [0]
    while shift >= 1:
        parts = parts + [lax.ppermute(p, "virt", [(d, d ^ shift) for d in range(columns)]) for p in parts]
        order = order + [o ^ shift for o in order]
        shift //= 2
    energies = virt_energy.reshape(columns, slab)
    row = jnp.concatenate(
        [lax.dynamic_slice_in_dim(energies, column ^ o, 1, 0) for o in order], axis=1
    )
    col = lax.dynamic_slice_in_dim(energies, column, 1, 0).reshape(slab, 1)

    total = aux * hosts
    step = next(c for c in (256, 128, 64, 32, 16) if total % c == 0)
    toward = pl.pallas_call(
        functools.partial(pair_kernel, hosts, per_host, columns, step),
        out_shape=[jax.ShapeDtypeStruct((aux, 2 * slab), jnp.bfloat16)] * hosts,
        in_specs=[in_smem, in_smem, in_smem, in_vmem, in_vmem] + [in_vmem] * columns,
        out_specs=[in_vmem] * hosts,
        scratch_shapes=[pltpu.VMEM((total, columns * slab), jnp.bfloat16)] * 2 + plan_scratch,
        name="pairs",
    )(table, here, occ_energy, col, row, *parts)

    returned = exchange(toward)
    return pl.pallas_call(
        functools.partial(scatter_kernel, hosts, per_host, orbitals, strips),
        grid=(steps,),
        out_shape=jax.ShapeDtypeStruct((slab, local), jnp.float32),
        in_specs=[in_smem, in_smem] + [pl.BlockSpec((block, 2 * slab), lambda g: (g, 0))] * hosts,
        out_specs=pl.BlockSpec((slab, width), lambda g: (0, g)),
        scratch_shapes=[sel_scratch] + plan_scratch,
        name="scatter",
    )(table, here, *returned)


def plain_body(hosts, columns, factors, occ_energy, virt_energy, pair_table, pair_count):
    per_host = pair_table.shape[0]
    tables = lax.all_gather(pair_table, "occ", axis=0, tiled=True)
    counts = lax.all_gather(pair_count, "occ", axis=0, tiled=True)
    entries = jnp.arange(hosts * per_host, dtype=jnp.int32)
    active = entries % per_host < jnp.repeat(counts, per_host)
    slot_count = -(-(per_host * hosts // 2) // hosts)
    ranking = jnp.cumsum(active.astype(jnp.int32)) - 1
    targets = jnp.arange(hosts * slot_count, dtype=jnp.int32)
    select = (active[None, :] & (ranking[None, :] == targets[:, None])).astype(jnp.int32)
    plan = jnp.sum(select[:, :, None] * tables[None, :, :], axis=1).reshape(hosts, slot_count, 2)
    enabled = jnp.max(select, axis=1).reshape(hosts, slot_count)
    column = lax.axis_index("virt")
    myself = lax.axis_index("occ")
    orbitals = occ_energy.shape[0]
    slab = factors.shape[0]
    aux = factors.shape[1] // orbitals
    own = lax.dynamic_slice_in_dim(virt_energy, column * slab, slab)
    cube = factors.reshape(slab, aux, orbitals)
    gamma = jnp.zeros((slab, aux, orbitals), jnp.float32)
    for position in range(slot_count):
        wanted = plan[:, position].T.reshape(-1)
        onehot = (wanted[:, None] == jnp.arange(orbitals, dtype=jnp.int32)[None, :]).astype(jnp.bfloat16)
        picked = lax.dot_general(
            cube, onehot, (((2,), (1,)), ((), ())), preferred_element_type=jnp.float32
        ).astype(jnp.bfloat16)
        outgoing = picked.reshape(slab, aux, 2, hosts)
        both = lax.all_to_all(outgoing, "occ", split_axis=3, concat_axis=1, tiled=True)
        both = lax.all_gather(both, "virt", axis=0, tiled=True)
        left, right = both[:, :, 0, 0], both[:, :, 1, 0]
        mine = lax.dynamic_index_in_dim(plan[:, position], myself, 0, keepdims=False)
        live = lax.dynamic_index_in_dim(enabled[:, position], myself, 0, keepdims=False).astype(jnp.float32)
        left_slab = lax.dynamic_slice_in_dim(left, column * slab, slab, 0)
        right_slab = lax.dynamic_slice_in_dim(right, column * slab, slab, 0)
        dims = (((1,), (1,)), ((), ()))
        rows = lax.dot_general(left_slab, right, dims, preferred_element_type=jnp.float32)
        cols = lax.dot_general(right_slab, left, dims, preferred_element_type=jnp.float32)
        energy = jnp.take(occ_energy, mine[0]) + jnp.take(occ_energy, mine[1])
        den = energy - own[:, None] - virt_energy[None, :]
        mixed_rows = ((2.0 * rows - cols) / den * live).astype(jnp.bfloat16)
        mixed_cols = ((2.0 * cols - rows) / den * live).astype(jnp.bfloat16)
        toward_first = jnp.dot(mixed_rows, right, preferred_element_type=jnp.float32)
        toward_second = jnp.dot(mixed_cols, left, preferred_element_type=jnp.float32)
        packed = jnp.stack([toward_first.astype(jnp.bfloat16), toward_second.astype(jnp.bfloat16)], axis=2)
        packed = packed.reshape(slab, hosts, aux, 2, 1)
        back = lax.all_to_all(packed, "occ", split_axis=1, concat_axis=4, tiled=True)
        gamma = gamma + lax.dot_general(
            back.reshape(slab, aux, 2 * hosts), onehot, (((2,), (0,)), ((), ())), preferred_element_type=jnp.float32
        )
    return gamma.reshape(factors.shape)


def solution(mesh):
    hosts, columns = mesh.shape["occ"], mesh.shape["virt"]

    def body(factors, occ_energy, virt_energy, pair_table, pair_count):
        slab, local = factors.shape
        orbitals = occ_energy.shape[0]
        fits = (
            hosts <= 8
            and hosts & (hosts - 1) == 0
            and columns & (columns - 1) == 0
            and pair_table.shape[0] == 2
            and (local // orbitals) % STRIP == 0
            and (STRIP * orbitals) % LANES == 0
            and (2 * slab) % LANES == 0
        )
        run = fast_body if fits else plain_body
        return run(hosts, columns, factors, occ_energy, virt_energy, pair_table, pair_count)

    in_specs = (P("virt", "occ"), P(), P(), P("occ", None), P("occ"))
    return jax.shard_map(body, mesh=mesh, in_specs=in_specs, out_specs=P("virt", "occ"), check_vma=False)
```

time: 397 us -> 128 us (0.32); the launches traced: 392 us -> 127 us
  waiting for transfers between devices: 223 us -> 70.4 us
  local copies, waits for them, and re-layouts: 88.5 us -> 4.91 us
  blocking collectives: 26.6 us -> 0 us
  Pallas kernels: 0 us -> 22.7 us
  between operations: 20.1 us -> 0.78 us
  starting transfers between devices: 12.4 us -> 26.3 us
  matrix products: 12 us -> 0 us
  other arithmetic: 9.26 us -> 2.22 us
    all_to_all x2 -> x0, waiting for transfers between devices: 129 us -> none  [the longest x1 94.3 us: one_slot(): lax.all_to_all(outgoing, 'occ', split_axis=3, concat_axis=1, tiled=True)]
    all_gather x1 -> x0, waiting for transfers between devices: 93.4 us -> none  [body(): source = lax.all_gather(factors, 'virt', axis=0, tiled=True)]
    ppermute x0 -> x20, waiting for transfers between devices: none -> 70.4 us  [the longest x14 39.4 us: exchange(): got[s] = lax.ppermute(pieces[s], 'occ', [(d, d ^ s) for d in range(hosts)])]
    reshape x7 -> x3, local copies, waits for them, and re-layouts: 37.7 us -> 1.59 us  [the longest x1 0.76 us: fast_body(): pair_table.reshape(1, -1)]
    ppermute x0 -> x20, starting transfers between devices: none -> 26.3 us  [the longest x14 20.6 us: exchange(): got[s] = lax.ppermute(pieces[s], 'occ', [(d, d ^ s) for d in range(hosts)])]
    all_gather x1 -> x0, local copies, waits for them, and re-layouts: 24.6 us -> none  [body(): source = lax.all_gather(factors, 'virt', axis=0, tiled=True)]
    pallas_call x0 -> x3, Pallas kernels: none -> 22.7 us  [the longest x1 8.93 us: fast_body(): pl.pallas_call(functools.partial(pair_kernel, hosts, per_host, columns, s...]
    all_gather x1 -> x0, blocking collectives: 16.1 us -> none  [body(): lax.all_gather(pair_table, 'occ', axis=0, tiled=True)]
  transfers between devices with their start and end apart: 3 -> 20, of which waited for: 3 -> 16; matrix products, arithmetic and copies ran while one was open for 1% -> 3% of each run, Pallas kernels for 0% -> 0%
where the time goes in v1:
time: 128 us; the launch traced here: 127 us
  waiting for transfers between devices  70.4 us (55%)
  starting transfers between devices  26.3 us (21%)
  Pallas kernels  22.7 us (18%)
  local copies, waits for them, and re-layouts  4.91 us (4%)
  other arithmetic  2.22 us (2%)
    ppermute x14, waiting for transfers between devices, exchange(): got[s] = lax.ppermute(pieces[s], 'occ', [(d, d ^ s) for d in range(hosts)])  39.4 us
    ppermute x3, waiting for transfers between devices, fast_body(): lax.ppermute(p, 'virt', [(d, d ^ shift) for d in range(columns)])  23.5 us
    ppermute x14, starting transfers between devices, exchange(): got[s] = lax.ppermute(pieces[s], 'occ', [(d, d ^ s) for d in range(hosts)])  20.6 us
    pallas_call x1, Pallas kernels, fast_body(): pl.pallas_call(functools.partial(pair_kernel, hosts, per_host, columns, s...  8.93 us
    ppermute x3, waiting for transfers between devices, fast_body(): other = lax.ppermute(table, 'occ', [(d, d ^ shift) for d in range(hosts)])  7.5 us
    pallas_call x1, Pallas kernels, fast_body(): pl.pallas_call(functools.partial(scatter_kernel, hosts, per_host, orbital...  7.14 us
    pallas_call x1, Pallas kernels, fast_body(): pl.pallas_call(functools.partial(select_kernel, hosts, per_host, orbitals...  6.67 us
    ppermute x3, starting transfers between devices, fast_body(): other = lax.ppermute(table, 'occ', [(d, d ^ shift) for d in range(hosts)])  4.12 us
  transfers between devices with their start and end apart: 20, of which 16 were waited for; matrix products, arithmetic and copies ran while one was open for 3% of the time, Pallas kernels for 0%

profile of v1, /device:TPU:8, one launch (start us, length us, event | category | flops | bytes accessed | tf_op | source)
XLA Modules:
  0.0 127.3 jit_solution(3610541271628193919)
XLA Ops:
  1.5 1.5 %collective-permute-start = (s32[1,5]{1,0:T(1,128)S(1)}, s32[1,5]{1,0:T(1,128)S(1)}, u32[]{:S(2)}, u32[]{:S(2)}) collective-permute-start(s32[1,5]{1,0:T(1,128)S(1)} %pad_add_fusion.3), channel_id=1, source_target_pairs={{0,4},{4,0},{8,12},{12,8},{16,20},{20,16},{24,28},{28,24},{1,5},{5... | collective-permute-start | bytes 68 | tf_op jit(solution)/shard_map/ppermute | solution.py:145
  3.0 2.0 %collective-permute-done = s32[1,5]{1,0:T(1,128)S(1)} collective-permute-done((s32[1,5]{1,0:T(1,128)S(1)}, s32[1,5]{1,0:T(1,128)S(1)}, u32[]{:S(2)}, u32[]{:S(2)}) %collective-permute-start) | collective-permute-done | bytes 52 | tf_op jit(solution)/shard_map/ppermute | solution.py:145
  5.1 3.6 %collective-permute-done.1 = s32[2,5]{1,0:T(2,128)S(1)} collective-permute-done((s32[2,5]{1,0:T(2,128)S(1)}, s32[2,5]{1,0:T(2,128)S(1)}, u32[]{:S(2)}, u32[]{:S(2)}) %collective-permute-start.1) | collective-permute-done | bytes 72 | tf_op jit(solution)/shard_map/ppermute | solution.py:145
  8.8 2.6 %collective-permute-start.2 = (s32[4,5]{1,0:T(4,128)S(1)}, s32[4,5]{1,0:T(4,128)S(1)}, u32[]{:S(2)}, u32[]{:S(2)}) collective-permute-start(s32[4,5]{1,0:T(4,128)S(1)} %pad_add_fusion.1), channel_id=1, source_target_pairs={{0,16},{4,20},{8,24},{12,28},{16,0},{20,4},{24,8},{28,12},{1,17},{... | collective-permute-start | bytes 248 | tf_op jit(solution)/shard_map/ppermute | solution.py:145
  11.4 1.9 %collective-permute-done.2 = s32[4,5]{1,0:T(4,128)S(1)} collective-permute-done((s32[4,5]{1,0:T(4,128)S(1)}, s32[4,5]{1,0:T(4,128)S(1)}, u32[]{:S(2)}, u32[]{:S(2)}) %collective-permute-start.2) | collective-permute-done | bytes 112 | tf_op jit(solution)/shard_map/ppermute | solution.py:145
  13.9 6.7 %select.1 = (bf16[192,384]{1,0:T(8,128)(2,1)}, bf16[192,384]{1,0:T(8,128)(2,1)}, bf16[192,384]{1,0:T(8,128)(2,1)}, bf16[192,384]{1,0:T(8,128)(2,1)}, bf16[192,38...) custom-call(s32[8,5]{1,0:T(8,128)} %pad_add_fusion.tab_ref, ...), custom_call_target="tpu_custom_call" | custom-call | tf_op jit(solution)/shard_map/select/pallas_call | solution.py:159
  20.6 1.6 %collective-permute-start.3 = (bf16[192,384]{1,0:T(8,128)(2,1)}, bf16[192,384]{1,0:T(8,128)(2,1)S(1)}, u32[]{:S(2)}, u32[]{:S(2)}) collective-permute-start(bf16[192,384]{1,0:T(8,128)(2,1)} %get-tuple-element.22), channel_id=1, source_target_pairs={{0,4},{4,0},{8,12},{12,8},{16,20},{20,16},{24,28},{28,24},{1,5},{5... | collective-permute-start | bytes 442376 | tf_op jit(solution)/shard_map/ppermute | solution.py:172
  22.6 1.5 %collective-permute-start.5 = (bf16[192,384]{1,0:T(8,128)(2,1)}, bf16[192,384]{1,0:T(8,128)(2,1)S(1)}, u32[]{:S(2)}, u32[]{:S(2)}) collective-permute-start(bf16[192,384]{1,0:T(8,128)(2,1)} %get-tuple-element.24), channel_id=1, source_target_pairs={{0,12},{4,8},{8,4},{12,0},{16,28},{20,24},{24,20},{28,16},{1,13},{... | collective-permute-start | bytes 442376 | tf_op jit(solution)/shard_map/ppermute | solution.py:172
  24.2 2.6 %collective-permute-start.6 = (bf16[192,384]{1,0:T(8,128)(2,1)}, bf16[192,384]{1,0:T(8,128)(2,1)S(1)}, u32[]{:S(2)}, u32[]{:S(2)}) collective-permute-start(bf16[192,384]{1,0:T(8,128)(2,1)} %get-tuple-element.25), channel_id=1, source_target_pairs={{0,16},{4,20},{8,24},{12,28},{16,0},{20,4},{24,8},{28,12},{1,17},{... | collective-permute-start | bytes 442376 | tf_op jit(solution)/shard_map/ppermute | solution.py:172
  26.7 1.3 %collective-permute-start.7 = (bf16[192,384]{1,0:T(8,128)(2,1)}, bf16[192,384]{1,0:T(8,128)(2,1)S(1)}, u32[]{:S(2)}, u32[]{:S(2)}) collective-permute-start(bf16[192,384]{1,0:T(8,128)(2,1)} %get-tuple-element.26), channel_id=1, source_target_pairs={{0,20},{4,16},{8,28},{12,24},{16,4},{20,0},{24,12},{28,8},{1,21},{... | collective-permute-start | bytes 442376 | tf_op jit(solution)/shard_map/ppermute | solution.py:172
  29.0 1.6 %collective-permute-start.8 = (bf16[192,384]{1,0:T(8,128)(2,1)}, bf16[192,384]{1,0:T(8,128)(2,1)S(1)}, u32[]{:S(2)}, u32[]{:S(2)}) collective-permute-start(bf16[192,384]{1,0:T(8,128)(2,1)} %get-tuple-element.27), channel_id=1, source_target_pairs={{0,24},{4,28},{8,16},{12,20},{16,8},{20,12},{24,0},{28,4},{1,25},{... | collective-permute-start | bytes 442376 | tf_op jit(solution)/shard_map/ppermute | solution.py:172
  32.2 8.5 %collective-permute-done.6 = bf16[192,384]{1,0:T(8,128)(2,1)S(1)} collective-permute-done((bf16[192,384]{1,0:T(8,128)(2,1)}, bf16[192,384]{1,0:T(8,128)(2,1)S(1)}, u32[]{:S(2)}, u32[]{:S(2)}) %collective-permute-start.6) | collective-permute-done | bytes 147488 | tf_op jit(solution)/shard_map/ppermute | solution.py:172
  40.8 3.1 %collective-permute-done.7 = bf16[192,384]{1,0:T(8,128)(2,1)S(1)} collective-permute-done((bf16[192,384]{1,0:T(8,128)(2,1)}, bf16[192,384]{1,0:T(8,128)(2,1)S(1)}, u32[]{:S(2)}, u32[]{:S(2)}) %collective-permute-start.7) | collective-permute-done | bytes 147488 | tf_op jit(solution)/shard_map/ppermute | solution.py:172
  44.0 3.4 %collective-permute-done.8 = bf16[192,384]{1,0:T(8,128)(2,1)S(1)} collective-permute-done((bf16[192,384]{1,0:T(8,128)(2,1)}, bf16[192,384]{1,0:T(8,128)(2,1)S(1)}, u32[]{:S(2)}, u32[]{:S(2)}) %collective-permute-start.8) | collective-permute-done | bytes 147488 | tf_op jit(solution)/shard_map/ppermute | solution.py:172
  47.4 1.9 %collective-permute-done.9 = bf16[192,384]{1,0:T(8,128)(2,1)S(1)} collective-permute-done((bf16[192,384]{1,0:T(8,128)(2,1)}, bf16[192,384]{1,0:T(8,128)(2,1)S(1)}, u32[]{:S(2)}, u32[]{:S(2)}) %collective-permute-start.9) | collective-permute-done | bytes 147488 | tf_op jit(solution)/shard_map/ppermute | solution.py:172
  49.3 1.6 %collective-permute-start.10 = (bf16[1536,384]{1,0:T(8,128)(2,1)S(1)}, bf16[1536,384]{1,0:T(8,128)(2,1)S(1)}, u32[]{:S(2)}, u32[]{:S(2)}) collective-permute-start(bf16[1536,384]{1,0:T(8,128)(2,1)S(1)} %constant_dynamic-update-slice_fusion.rest_0_), channel_id=1, source_target_pairs={{0,2},{1,3},{2,0},{3,1},{4,6},{5,7},{6,4},{7,5},{8,10},{9,11},{10,... | collective-permute-start | bytes 3538952 | tf_op jit(solution)/shard_map/ppermute | solution.py:181
  50.9 23.4 %collective-permute-done.10.rest_1_ = bf16[1536,384]{1,0:T(8,128)(2,1)S(1)} collective-permute-done((bf16[1536,384]{1,0:T(8,128)(2,1)S(1)}, bf16[1536,384]{1,0:T(8,128)(2,1)S(1)}, u32[]{:S(2)}, u32[]{:S(2)}) %collective-permute-start.10) | collective-permute-done | bytes 1179680 | tf_op jit(solution)/shard_map/ppermute | solution.py:181
  75.8 1.3 %pad_maximum_fusion.row_ref = f32[1,768]{1,0:T(1,128)} fusion(f32[1,192]{1,0:T(1,128)S(1)} %get-tuple-element.38, f32[1,192]{1,0:T(1,128)} %get-tuple-element.39, f32[1,192]{1,0:T(1,128)S(1)} %get-tuple-element.37, f32[1,192]{1,0:T(1,128)S(1)} %get-tuple-element.40), kind=kLoop, calls=%fused_computation.9 | loop fusion | flops 2304 | bytes 6144 | tf_op jit(solution)/shard_map/concatenate | solution.py:185
  78.1 8.9 %pairs.1 = (bf16[192,384]{1,0:T(8,128)(2,1)}, bf16[192,384]{1,0:T(8,128)(2,1)}, bf16[192,384]{1,0:T(8,128)(2,1)}, bf16[192,384]{1,0:T(8,128)(2,1)}, bf16[192,384...) custom-call(s32[8,5]{1,0:T(8,128)} %pad_add_fusion.tab_ref, ...), custom_call_target="tpu_custom_call" | custom-call | tf_op jit(solution)/shard_map/pairs/pallas_call | solution.py:192
  87.1 2.1 %collective-permute-start.13 = (bf16[192,384]{1,0:T(8,128)(2,1)}, bf16[192,384]{1,0:T(8,128)(2,1)S(1)}, u32[]{:S(2)}, u32[]{:S(2)}) collective-permute-start(bf16[192,384]{1,0:T(8,128)(2,1)} %get-tuple-element.30), channel_id=1, source_target_pairs={{0,4},{4,0},{8,12},{12,8},{16,20},{20,16},{24,28},{28,24},{1,5},{5... | collective-permute-start | bytes 442376 | tf_op jit(solution)/shard_map/ppermute | solution.py:172
  89.2 1.5 %collective-permute-start.15 = (bf16[192,384]{1,0:T(8,128)(2,1)}, bf16[192,384]{1,0:T(8,128)(2,1)S(1)}, u32[]{:S(2)}, u32[]{:S(2)}) collective-permute-start(bf16[192,384]{1,0:T(8,128)(2,1)} %get-tuple-element.32), channel_id=1, source_target_pairs={{0,12},{4,8},{8,4},{12,0},{16,28},{20,24},{24,20},{28,16},{1,13},{... | collective-permute-start | bytes 442376 | tf_op jit(solution)/shard_map/ppermute | solution.py:172
  90.7 2.0 %collective-permute-start.16 = (bf16[192,384]{1,0:T(8,128)(2,1)}, bf16[192,384]{1,0:T(8,128)(2,1)S(1)}, u32[]{:S(2)}, u32[]{:S(2)}) collective-permute-start(bf16[192,384]{1,0:T(8,128)(2,1)} %get-tuple-element.33), channel_id=1, source_target_pairs={{0,16},{4,20},{8,24},{12,28},{16,0},{20,4},{24,8},{28,12},{1,17},{... | collective-permute-start | bytes 442376 | tf_op jit(solution)/shard_map/ppermute | solution.py:172
  92.7 2.3 %collective-permute-start.17 = (bf16[192,384]{1,0:T(8,128)(2,1)}, bf16[192,384]{1,0:T(8,128)(2,1)S(1)}, u32[]{:S(2)}, u32[]{:S(2)}) collective-permute-start(bf16[192,384]{1,0:T(8,128)(2,1)} %get-tuple-element.34), channel_id=1, source_target_pairs={{0,20},{4,16},{8,28},{12,24},{16,4},{20,0},{24,12},{28,8},{1,21},{... | collective-permute-start | bytes 442376 | tf_op jit(solution)/shard_map/ppermute | solution.py:172
  95.0 1.1 collective-permute-start.18
  96.2 1.9 %collective-permute-done.14.rest_2_ = bf16[192,384]{1,0:T(8,128)(2,1)S(1)} collective-permute-done((bf16[192,384]{1,0:T(8,128)(2,1)}, bf16[192,384]{1,0:T(8,128)(2,1)S(1)}, u32[]{:S(2)}, u32[]{:S(2)}) %collective-permute-start.14) | collective-permute-done | bytes 147488 | tf_op jit(solution)/shard_map/ppermute | solution.py:172
  98.1 2.0 %collective-permute-start.19 = (bf16[192,384]{1,0:T(8,128)(2,1)}, bf16[192,384]{1,0:T(8,128)(2,1)S(1)}, u32[]{:S(2)}, u32[]{:S(2)}) collective-permute-start(bf16[192,384]{1,0:T(8,128)(2,1)} %get-tuple-element.36), channel_id=1, source_target_pairs={{0,28},{4,24},{8,20},{12,16},{16,12},{20,8},{24,4},{28,0},{1,29},{... | collective-permute-start | bytes 442376 | tf_op jit(solution)/shard_map/ppermute | solution.py:172
  100.0 1.4 %collective-permute-done.15.rest_3_ = bf16[192,384]{1,0:T(8,128)(2,1)S(1)} collective-permute-done((bf16[192,384]{1,0:T(8,128)(2,1)}, bf16[192,384]{1,0:T(8,128)(2,1)S(1)}, u32[]{:S(2)}, u32[]{:S(2)}) %collective-permute-start.15) | collective-permute-done | bytes 147488 | tf_op jit(solution)/shard_map/ppermute | solution.py:172
  101.4 1.6 %collective-permute-done.16.rest_4_ = bf16[192,384]{1,0:T(8,128)(2,1)S(1)} collective-permute-done((bf16[192,384]{1,0:T(8,128)(2,1)}, bf16[192,384]{1,0:T(8,128)(2,1)S(1)}, u32[]{:S(2)}, u32[]{:S(2)}) %collective-permute-start.16) | collective-permute-done | bytes 147488 | tf_op jit(solution)/shard_map/ppermute | solution.py:172
  103.0 10.0 %collective-permute-done.17.rest_5_ = bf16[192,384]{1,0:T(8,128)(2,1)S(1)} collective-permute-done((bf16[192,384]{1,0:T(8,128)(2,1)}, bf16[192,384]{1,0:T(8,128)(2,1)S(1)}, u32[]{:S(2)}, u32[]{:S(2)}) %collective-permute-start.17) | collective-permute-done | bytes 147488 | tf_op jit(solution)/shard_map/ppermute | solution.py:172
  113.1 4.0 %collective-permute-done.18.rest_6_ = bf16[192,384]{1,0:T(8,128)(2,1)S(1)} collective-permute-done((bf16[192,384]{1,0:T(8,128)(2,1)}, bf16[192,384]{1,0:T(8,128)(2,1)S(1)}, u32[]{:S(2)}, u32[]{:S(2)}) %collective-permute-start.18) | collective-permute-done | bytes 147488 | tf_op jit(solution)/shard_map/ppermute | solution.py:172
  117.0 2.5 %collective-permute-done.19.rest_7_ = bf16[192,384]{1,0:T(8,128)(2,1)S(1)} collective-permute-done((bf16[192,384]{1,0:T(8,128)(2,1)}, bf16[192,384]{1,0:T(8,128)(2,1)S(1)}, u32[]{:S(2)}, u32[]{:S(2)}) %collective-permute-start.19) | collective-permute-done | bytes 147488 | tf_op jit(solution)/shard_map/ppermute | solution.py:172
  120.2 7.1 %scatter.1 = f32[192,12288]{1,0:T(8,128)} custom-call(s32[8,5]{1,0:T(8,128)} %pad_add_fusion.tab_ref, s32[1]{0:T(128)} %bitcast.1.me_ref, bf16[192,384]{1,0:T(8,128)(2,1)} %get-tuple-element.29.rest_0_, bf16[192,384]{1,0:T(8,128)(2,1)} %copy-done.3, bf16[192,384]{1,0:T(8,128)(2,1)} %copy-done.4, bf16[192,384]{1,0:T(8,128)(2,1)} %copy-done.5, ...), custom_call_target="tpu_custom_call" | custom-call | tf_op jit(solution)/shard_map/scatter/pallas_call | solution.py:202
  (50 shorter events, 7.9 us)
Async XLA Ops:
  1.5 3.6 %collective-permute-start = (s32[1,5]{1,0:T(1,128)S(1)}, s32[1,5]{1,0:T(1,128)S(1)}, u32[]{:S(2)}, u32[]{:S(2)}) collective-permute-start(s32[1,5]{1,0:T(1,128)S(1)} %pad_add_fusion.3), channel_id=1, source_target_pairs={{0,4},{4,0},{8,12},{12,8},{16,20},{20,16},{24,28},{28,24},{1,5},{5... | collective-permute-start | bytes 68 | tf_op jit(solution)/shard_map/ppermute | solution.py:145
  5.1 3.6 %collective-permute-start.1 = (s32[2,5]{1,0:T(2,128)S(1)}, s32[2,5]{1,0:T(2,128)S(1)}, u32[]{:S(2)}, u32[]{:S(2)}) collective-permute-start(s32[2,5]{1,0:T(2,128)S(1)} %pad_add_fusion.2), channel_id=1, source_target_pairs={{0,8},{4,12},{8,0},{12,4},{16,24},{20,28},{24,16},{28,20},{1,9},{5... | collective-permute-start | bytes 128 | tf_op jit(solution)/shard_map/ppermute | solution.py:145
  8.8 4.5 %collective-permute-start.2 = (s32[4,5]{1,0:T(4,128)S(1)}, s32[4,5]{1,0:T(4,128)S(1)}, u32[]{:S(2)}, u32[]{:S(2)}) collective-permute-start(s32[4,5]{1,0:T(4,128)S(1)} %pad_add_fusion.1), channel_id=1, source_target_pairs={{0,16},{4,20},{8,24},{12,28},{16,0},{20,4},{24,8},{28,12},{1,17},{... | collective-permute-start | bytes 248 | tf_op jit(solution)/shard_map/ppermute | solution.py:145
  20.6 8.4 %collective-permute-start.3 = (bf16[192,384]{1,0:T(8,128)(2,1)}, bf16[192,384]{1,0:T(8,128)(2,1)S(1)}, u32[]{:S(2)}, u32[]{:S(2)}) collective-permute-start(bf16[192,384]{1,0:T(8,128)(2,1)} %get-tuple-element.22), channel_id=1, source_target_pairs={{0,4},{4,0},{8,12},{12,8},{16,20},{20,16},{24,28},{28,24},{1,5},{5... | collective-permute-start | bytes 442376 | tf_op jit(solution)/shard_map/ppermute | solution.py:172
  22.2 8.5 %collective-permute-start.4 = (bf16[192,384]{1,0:T(8,128)(2,1)}, bf16[192,384]{1,0:T(8,128)(2,1)S(1)}, u32[]{:S(2)}, u32[]{:S(2)}) collective-permute-start(bf16[192,384]{1,0:T(8,128)(2,1)} %get-tuple-element.23), channel_id=1, source_target_pairs={{0,8},{4,12},{8,0},{12,4},{16,24},{20,28},{24,16},{28,20},{1,9},{5... | collective-permute-start | bytes 442376 | tf_op jit(solution)/shard_map/ppermute | solution.py:172
  22.6 9.6 %collective-permute-start.5 = (bf16[192,384]{1,0:T(8,128)(2,1)}, bf16[192,384]{1,0:T(8,128)(2,1)S(1)}, u32[]{:S(2)}, u32[]{:S(2)}) collective-permute-start(bf16[192,384]{1,0:T(8,128)(2,1)} %get-tuple-element.24), channel_id=1, source_target_pairs={{0,12},{4,8},{8,4},{12,0},{16,28},{20,24},{24,20},{28,16},{1,13},{... | collective-permute-start | bytes 442376 | tf_op jit(solution)/shard_map/ppermute | solution.py:172
  24.2 16.6 %collective-permute-start.6 = (bf16[192,384]{1,0:T(8,128)(2,1)}, bf16[192,384]{1,0:T(8,128)(2,1)S(1)}, u32[]{:S(2)}, u32[]{:S(2)}) collective-permute-start(bf16[192,384]{1,0:T(8,128)(2,1)} %get-tuple-element.25), channel_id=1, source_target_pairs={{0,16},{4,20},{8,24},{12,28},{16,0},{20,4},{24,8},{28,12},{1,17},{... | collective-permute-start | bytes 442376 | tf_op jit(solution)/shard_map/ppermute | solution.py:172
  26.7 17.2 %collective-permute-start.7 = (bf16[192,384]{1,0:T(8,128)(2,1)}, bf16[192,384]{1,0:T(8,128)(2,1)S(1)}, u32[]{:S(2)}, u32[]{:S(2)}) collective-permute-start(bf16[192,384]{1,0:T(8,128)(2,1)} %get-tuple-element.26), channel_id=1, source_target_pairs={{0,20},{4,16},{8,28},{12,24},{16,4},{20,0},{24,12},{28,8},{1,21},{... | collective-permute-start | bytes 442376 | tf_op jit(solution)/shard_map/ppermute | solution.py:172
  28.0 46.2 %copy-start.10 = (f32[768]{0:T(1024)S(1)}, f32[768]{0:T(1024)}, u32[]{:S(2)}) copy-start(f32[768]{0:T(1024)} %param.7) | copy-start | bytes 9220
  29.0 18.4 %collective-permute-start.8 = (bf16[192,384]{1,0:T(8,128)(2,1)}, bf16[192,384]{1,0:T(8,128)(2,1)S(1)}, u32[]{:S(2)}, u32[]{:S(2)}) collective-permute-start(bf16[192,384]{1,0:T(8,128)(2,1)} %get-tuple-element.27), channel_id=1, source_target_pairs={{0,24},{4,28},{8,16},{12,20},{16,8},{20,12},{24,0},{28,4},{1,25},{... | collective-permute-start | bytes 442376 | tf_op jit(solution)/shard_map/ppermute | solution.py:172
  30.7 18.6 %collective-permute-start.9 = (bf16[192,384]{1,0:T(8,128)(2,1)}, bf16[192,384]{1,0:T(8,128)(2,1)S(1)}, u32[]{:S(2)}, u32[]{:S(2)}) collective-permute-start(bf16[192,384]{1,0:T(8,128)(2,1)} %get-tuple-element.28), channel_id=1, source_target_pairs={{0,28},{4,24},{8,20},{12,16},{16,12},{20,8},{24,4},{28,0},{1,29},{... | collective-permute-start | bytes 442376 | tf_op jit(solution)/shard_map/ppermute | solution.py:172
  49.3 27.9 %copy-start = (bf16[1536,384]{1,0:T(8,128)(2,1)}, bf16[1536,384]{1,0:T(8,128)(2,1)S(1)}, u32[]{:S(2)}) copy-start(bf16[1536,384]{1,0:T(8,128)(2,1)S(1)} %constant_dynamic-update-slice_fusion.rest_0_) | copy-start | bytes 3538948
  49.3 24.9 %collective-permute-start.10 = (bf16[1536,384]{1,0:T(8,128)(2,1)S(1)}, bf16[1536,384]{1,0:T(8,128)(2,1)S(1)}, u32[]{:S(2)}, u32[]{:S(2)}) collective-permute-start(bf16[1536,384]{1,0:T(8,128)(2,1)S(1)} %constant_dynamic-update-slice_fusion.rest_0_), channel_id=1, source_target_pairs={{0,2},{1,3},{2,0},{3,1},{4,6},{5,7},{6,4},{7,5},{8,10},{9,11},{10,... | collective-permute-start | bytes 3538952 | tf_op jit(solution)/shard_map/ppermute | solution.py:181
  50.9 26.2 %collective-permute-start.11 = (bf16[1536,384]{1,0:T(8,128)(2,1)S(1)}, bf16[1536,384]{1,0:T(8,128)(2,1)S(1)}, u32[]{:S(2)}, u32[]{:S(2)}) collective-permute-start(bf16[1536,384]{1,0:T(8,128)(2,1)S(1)} %constant_dynamic-update-slice_fusion.rest_0_), channel_id=1, source_target_pairs={{0,1},{1,0},{2,3},{3,2},{4,5},{5,4},{6,7},{7,6},{8,9},{9,8},{10,11... | collective-permute-start | bytes 3538952 | tf_op jit(solution)/shard_map/ppermute | solution.py:181
  74.3 3.0 %copy-start.1 = (bf16[1536,384]{1,0:T(8,128)(2,1)}, bf16[1536,384]{1,0:T(8,128)(2,1)S(1)}, u32[]{:S(2)}) copy-start(bf16[1536,384]{1,0:T(8,128)(2,1)S(1)} %collective-permute-done.10.rest_1_) | copy-start | bytes 3538948
  74.3 3.0 %collective-permute-start.12 = (bf16[1536,384]{1,0:T(8,128)(2,1)S(1)}, bf16[1536,384]{1,0:T(8,128)(2,1)}, u32[]{:S(2)}, u32[]{:S(2)}) collective-permute-start(bf16[1536,384]{1,0:T(8,128)(2,1)S(1)} %collective-permute-done.10.rest_1_), channel_id=1, source_target_pairs={{0,1},{1,0},{2,3},{3,2},{4,5},{5,4},{6,7},{7,6},{8,9},{9,8},{10,11... | collective-permute-start | bytes 3538952 | tf_op jit(solution)/shard_map/ppermute | solution.py:181
  77.1 1.0 copy-start.2
  87.1 8.0 %collective-permute-start.13 = (bf16[192,384]{1,0:T(8,128)(2,1)}, bf16[192,384]{1,0:T(8,128)(2,1)S(1)}, u32[]{:S(2)}, u32[]{:S(2)}) collective-permute-start(bf16[192,384]{1,0:T(8,128)(2,1)} %get-tuple-element.30), channel_id=1, source_target_pairs={{0,4},{4,0},{8,12},{12,8},{16,20},{20,16},{24,28},{28,24},{1,5},{5... | collective-permute-start | bytes 442376 | tf_op jit(solution)/shard_map/ppermute | solution.py:172
  89.2 8.9 %collective-permute-start.14 = (bf16[192,384]{1,0:T(8,128)(2,1)}, bf16[192,384]{1,0:T(8,128)(2,1)S(1)}, u32[]{:S(2)}, u32[]{:S(2)}) collective-permute-start(bf16[192,384]{1,0:T(8,128)(2,1)} %get-tuple-element.31), channel_id=1, source_target_pairs={{0,8},{4,12},{8,0},{12,4},{16,24},{20,28},{24,16},{28,20},{1,9},{5... | collective-permute-start | bytes 442376 | tf_op jit(solution)/shard_map/ppermute | solution.py:172
  89.2 12.2 %collective-permute-start.15 = (bf16[192,384]{1,0:T(8,128)(2,1)}, bf16[192,384]{1,0:T(8,128)(2,1)S(1)}, u32[]{:S(2)}, u32[]{:S(2)}) collective-permute-start(bf16[192,384]{1,0:T(8,128)(2,1)} %get-tuple-element.32), channel_id=1, source_target_pairs={{0,12},{4,8},{8,4},{12,0},{16,28},{20,24},{24,20},{28,16},{1,13},{... | collective-permute-start | bytes 442376 | tf_op jit(solution)/shard_map/ppermute | solution.py:172
  90.7 12.3 %collective-permute-start.16 = (bf16[192,384]{1,0:T(8,128)(2,1)}, bf16[192,384]{1,0:T(8,128)(2,1)S(1)}, u32[]{:S(2)}, u32[]{:S(2)}) collective-permute-start(bf16[192,384]{1,0:T(8,128)(2,1)} %get-tuple-element.33), channel_id=1, source_target_pairs={{0,16},{4,20},{8,24},{12,28},{16,0},{20,4},{24,8},{28,12},{1,17},{... | collective-permute-start | bytes 442376 | tf_op jit(solution)/shard_map/ppermute | solution.py:172
  92.7 20.4 %collective-permute-start.17 = (bf16[192,384]{1,0:T(8,128)(2,1)}, bf16[192,384]{1,0:T(8,128)(2,1)S(1)}, u32[]{:S(2)}, u32[]{:S(2)}) collective-permute-start(bf16[192,384]{1,0:T(8,128)(2,1)} %get-tuple-element.34), channel_id=1, source_target_pairs={{0,20},{4,16},{8,28},{12,24},{16,4},{20,0},{24,12},{28,8},{1,21},{... | collective-permute-start | bytes 442376 | tf_op jit(solution)/shard_map/ppermute | solution.py:172
  95.0 24.5 %copy-start.3 = (bf16[192,384]{1,0:T(8,128)(2,1)}, bf16[192,384]{1,0:T(8,128)(2,1)S(1)}, u32[]{:S(2)}) copy-start(bf16[192,384]{1,0:T(8,128)(2,1)S(1)} %collective-permute-done.13.rest_1_) | copy-start | bytes 442372
  95.0 22.0 %collective-permute-start.18 = (bf16[192,384]{1,0:T(8,128)(2,1)}, bf16[192,384]{1,0:T(8,128)(2,1)S(1)}, u32[]{:S(2)}, u32[]{:S(2)}) collective-permute-start(bf16[192,384]{1,0:T(8,128)(2,1)} %get-tuple-element.35), channel_id=1, source_target_pairs={{0,24},{4,28},{8,16},{12,20},{16,8},{20,12},{24,0},{28,4},{1,25},{... | collective-permute-start | bytes 442376 | tf_op jit(solution)/shard_map/ppermute | solution.py:172
  98.1 21.5 %copy-start.4 = (bf16[192,384]{1,0:T(8,128)(2,1)}, bf16[192,384]{1,0:T(8,128)(2,1)S(1)}, u32[]{:S(2)}) copy-start(bf16[192,384]{1,0:T(8,128)(2,1)S(1)} %collective-permute-done.14.rest_2_) | copy-start | bytes 442372
  98.1 21.4 %collective-permute-start.19 = (bf16[192,384]{1,0:T(8,128)(2,1)}, bf16[192,384]{1,0:T(8,128)(2,1)S(1)}, u32[]{:S(2)}, u32[]{:S(2)}) collective-permute-start(bf16[192,384]{1,0:T(8,128)(2,1)} %get-tuple-element.36), channel_id=1, source_target_pairs={{0,28},{4,24},{8,20},{12,16},{16,12},{20,8},{24,4},{28,0},{1,29},{... | collective-permute-start | bytes 442376 | tf_op jit(solution)/shard_map/ppermute | solution.py:172
  101.4 18.1 %copy-start.5 = (bf16[192,384]{1,0:T(8,128)(2,1)}, bf16[192,384]{1,0:T(8,128)(2,1)S(1)}, u32[]{:S(2)}) copy-start(bf16[192,384]{1,0:T(8,128)(2,1)S(1)} %collective-permute-done.15.rest_3_) | copy-start | bytes 442372
  103.0 16.5 %copy-start.6 = (bf16[192,384]{1,0:T(8,128)(2,1)}, bf16[192,384]{1,0:T(8,128)(2,1)S(1)}, u32[]{:S(2)}) copy-start(bf16[192,384]{1,0:T(8,128)(2,1)S(1)} %collective-permute-done.16.rest_4_) | copy-start | bytes 442372
  113.1 6.5 %copy-start.7 = (bf16[192,384]{1,0:T(8,128)(2,1)}, bf16[192,384]{1,0:T(8,128)(2,1)S(1)}, u32[]{:S(2)}) copy-start(bf16[192,384]{1,0:T(8,128)(2,1)S(1)} %collective-permute-done.17.rest_5_) | copy-start | bytes 442372
  117.0 2.5 %copy-start.8 = (bf16[192,384]{1,0:T(8,128)(2,1)}, bf16[192,384]{1,0:T(8,128)(2,1)S(1)}, u32[]{:S(2)}) copy-start(bf16[192,384]{1,0:T(8,128)(2,1)S(1)} %collective-permute-done.18.rest_6_) | copy-start | bytes 442372
  119.5 0.7 copy-start.9

commit v2 on v1

v2 whole, which is shorter than its diff:
```python
import functools

import jax
import jax.numpy as jnp
from jax import lax
from jax.experimental import pallas as pl
from jax.experimental.pallas import tpu as pltpu
from jax.sharding import PartitionSpec as P

LANES = 128
STRIP = 16
SELECT_BYTES = 24 * 1024 * 1024


def read_plan(tab_refs, me, hosts, per_host, first_ref, second_ref):
    tab_ref = tab_refs
    for t in range(hosts):
        first_ref[t] = jnp.int32(-1)
        second_ref[t] = jnp.int32(-1)
    rank = jnp.int32(0)
    for h in range(hosts):
        slot = h ^ me
        count = tab_ref[slot, 2 * per_host]
        for r in range(per_host):
            live = (r < count) & (rank < hosts)

            @pl.when(live)
            def _(rank=rank, r=r, slot=slot):
                first_ref[rank] = tab_ref[slot, 2 * r]
                second_ref[rank] = tab_ref[slot, 2 * r + 1]

            rank = rank + live.astype(jnp.int32)


def pick_matrix(first_ref, second_ref, me, hosts, orbitals, strip, sel_ref):
    width = strip * orbitals
    lane = lax.broadcasted_iota(jnp.int32, (strip, width), 1)
    row = lax.broadcasted_iota(jnp.int32, (strip, width), 0)
    here = lane - row * orbitals
    for s in range(hosts):
        for which, ref in enumerate((first_ref, second_ref)):
            orbital = ref[me ^ s]
            hit = (here == orbital) & (orbital >= 0)
            base = (which * hosts + s) * strip
            sel_ref[base:base + strip, :] = jnp.where(hit, 1.0, 0.0).astype(jnp.bfloat16)


def select_kernel(hosts, per_host, orbitals, tab_ref, ids_ref, x_ref, *rest):
    outs, (sel_ref, first_ref, second_ref) = rest[:hosts], rest[hosts:]
    me = ids_ref[0]
    read_plan(tab_ref, me, hosts, per_host, first_ref, second_ref)
    half = STRIP // 2
    pick_matrix(first_ref, second_ref, me, hosts, orbitals, half, sel_ref)
    width = half * orbitals
    aux = x_ref.shape[1] // orbitals
    for k in range(aux // STRIP):
        two = [
            lax.dot_general(
                sel_ref[...], x_ref[:, (2 * k + u) * width:(2 * k + u + 1) * width], (((1,), (1,)), ((), ())),
                preferred_element_type=jnp.float32,
            )
            for u in range(2)
        ]
        for s in range(hosts):
            left = jnp.concatenate([t[s * half:(s + 1) * half] for t in two], axis=0)
            right = jnp.concatenate([t[(hosts + s) * half:(hosts + s + 1) * half] for t in two], axis=0)
            outs[s][k * STRIP:(k + 1) * STRIP, :] = jnp.concatenate(
                [left.astype(jnp.bfloat16), right.astype(jnp.bfloat16)], axis=1
            )


def scatter_kernel(hosts, per_host, orbitals, strips, tab_ref, ids_ref, *rest):
    ins, (out_ref, sel_ref, first_ref, second_ref) = rest[:hosts], rest[hosts:]
    me = ids_ref[0]

    @pl.when(pl.program_id(0) == 0)
    def _():
        read_plan(tab_ref, me, hosts, per_host, first_ref, second_ref)
        pick_matrix(first_ref, second_ref, me, hosts, orbitals, STRIP, sel_ref)

    width = STRIP * orbitals
    slab = out_ref.shape[0]
    for k in range(strips):
        rows = [ins[s][k * STRIP:(k + 1) * STRIP, :] for s in range(hosts)]
        stacked = jnp.concatenate([r[:, :slab] for r in rows] + [r[:, slab:] for r in rows], axis=0)
        out_ref[:, k * width:(k + 1) * width] = lax.dot_general(
            stacked, sel_ref[...], (((0,), (0,)), ((), ())), preferred_element_type=jnp.float32
        )


def side_by_side(parts, rows, slab):
    blocks = [p[rows, :] for p in parts]
    return (
        jnp.concatenate([b[:, :slab] for b in blocks], axis=1),
        jnp.concatenate([b[:, slab:] for b in blocks], axis=1),
    )


def couple_chunks(parts, slab, step, one_ref, two_ref, lall=None, rall=None):
    dims = (((0,), (0,)), ((), ()))
    for c in range(parts[0].shape[0] // step):
        rows = slice(c * step, (c + 1) * step)
        left, right = side_by_side(parts, rows, slab)
        if lall is not None:
            lall[rows, :] = left
            rall[rows, :] = right
        one_ref[...] += lax.dot_general(left[:, :slab], right, dims, preferred_element_type=jnp.float32)
        two_ref[...] += lax.dot_general(right[:, :slab], left, dims, preferred_element_type=jnp.float32)


def toward_chunks(lefts, rights, mixed_rows, mixed_cols, out):
    dims = (((1,), (1,)), ((), ()))
    first = lax.dot_general(rights, mixed_rows, dims, preferred_element_type=jnp.float32)
    second = lax.dot_general(lefts, mixed_cols, dims, preferred_element_type=jnp.float32)
    out[...] = jnp.concatenate([first.astype(jnp.bfloat16), second.astype(jnp.bfloat16)], axis=1)


def near_kernel(groups, slab, step, *rest):
    parts, (one_ref, two_ref) = rest[:groups], rest[groups:]
    one_ref[...] = jnp.zeros_like(one_ref)
    two_ref[...] = jnp.zeros_like(two_ref)
    couple_chunks(parts, slab, step, one_ref, two_ref)


def far_kernel(hosts, per_host, order, slab, aux, step, tab_ref, ids_ref, occ_ref, virt_ref, one_in, two_in, *rest):
    groups = len(order)
    count = rest[0].shape[0] // aux
    parts, rest = rest[:groups], rest[groups:]
    outs, rest = rest[:count], rest[count:]
    rows_ref, cols_ref, one_ref, two_ref, lall, rall, first_ref, second_ref = rest
    me, column = ids_ref[0], ids_ref[1]
    read_plan(tab_ref, me, hosts, per_host, first_ref, second_ref)
    i, j = first_ref[me], second_ref[me]
    live = jnp.where(i >= 0, 1.0, 0.0)
    energy = occ_ref[jnp.maximum(i, 0)] + occ_ref[jnp.maximum(j, 0)]
    one_ref[...] = one_in[...]
    two_ref[...] = two_in[...]
    couple_chunks(parts, slab, step, one_ref, two_ref, lall, rall)
    bands = [virt_ref[:, g * slab:(g + 1) * slab] for g in range(groups)]

    def band(at):
        chosen = bands[0]
        for g in range(1, groups):
            chosen = jnp.where(at == g, bands[g], chosen)
        return chosen

    row = jnp.concatenate([band(column ^ o) for o in order], axis=1)
    col = jnp.transpose(jnp.broadcast_to(band(column), (LANES, slab)))[:, :1]
    den = energy - col - row
    one, two = one_ref[...], two_ref[...]
    rows_ref[...] = (((2.0 * one - two) / den) * live).astype(jnp.bfloat16)
    cols_ref[...] = (((2.0 * two - one) / den) * live).astype(jnp.bfloat16)
    for s in range(count):
        span = slice(s * aux, (s + 1) * aux)
        toward_chunks(lall[span, :], rall[span, :], rows_ref[...], cols_ref[...], outs[s])


def rest_kernel(groups, slab, aux, rows_ref, cols_ref, *rest):
    parts, outs = rest[:groups], rest[groups:]
    for s, out in enumerate(outs):
        left, right = side_by_side(parts, slice(s * aux, (s + 1) * aux), slab)
        toward_chunks(left, right, rows_ref[...], cols_ref[...], out)


def fast_body(hosts, columns, factors, occ_energy, virt_energy, pair_table, pair_count):
    slab, local = factors.shape
    orbitals = occ_energy.shape[0]
    aux = local // orbitals
    per_host = pair_table.shape[0]
    me = lax.axis_index("occ").astype(jnp.int32)
    column = lax.axis_index("virt").astype(jnp.int32)

    table = jnp.concatenate([pair_table.reshape(1, -1), pair_count.reshape(1, 1)], axis=1)
    shift = 1
    while shift < hosts:
        other = lax.ppermute(table, "occ", [(d, d ^ shift) for d in range(hosts)])
        table = jnp.concatenate([table, other], axis=0)
        shift *= 2
    ids = jnp.stack([me, column])

    plan_scratch = [pltpu.SMEM((hosts,), jnp.int32), pltpu.SMEM((hosts,), jnp.int32)]
    in_smem = pl.BlockSpec(memory_space=pltpu.SMEM)
    in_vmem = pl.BlockSpec(memory_space=pltpu.VMEM)
    piece = jax.ShapeDtypeStruct((aux, 2 * slab), jnp.bfloat16)
    bf16, f32 = jnp.bfloat16, jnp.float32
    full = columns * slab

    sent = pl.pallas_call(
        functools.partial(select_kernel, hosts, per_host, orbitals),
        out_shape=[piece] * hosts,
        in_specs=[in_smem, in_smem, in_vmem],
        out_specs=[in_vmem] * hosts,
        scratch_shapes=[pltpu.VMEM((hosts * STRIP, STRIP // 2 * orbitals), bf16)] + plan_scratch,
        compiler_params=pltpu.CompilerParams(vmem_limit_bytes=SELECT_BYTES),
        name="select",
    )(table, ids, factors)

    def over_occ(x, s):
        return lax.ppermute(x, "occ", [(d, d ^ s) for d in range(hosts)])

    def over_virt(x, s):
        return lax.ppermute(x, "virt", [(d, d ^ s) for d in range(columns)])

    def spread(x):
        parts, order = [x], [0]
        shift = columns // 2
        while shift >= 1:
            parts = parts + [over_virt(p, shift) for p in parts]
            order = order + [o ^ shift for o in order]
            shift //= 2
        return parts, order

    cut = hosts // 2
    got = {0: sent[0]}
    for s in reversed(range(1, hosts)):
        got[s] = over_occ(sent[s], s)
    near, order = spread(jnp.concatenate([got[s] for s in range(cut)], axis=0))
    far, _ = spread(jnp.concatenate([got[s] for s in range(cut, hosts)], axis=0))

    span = cut * aux
    step = next(c for c in (256, 128, 64, 32, 16) if span % c == 0)
    square = jax.ShapeDtypeStruct((slab, full), f32)
    flops = 4 * slab * full * span
    one, two = pl.pallas_call(
        functools.partial(near_kernel, columns, slab, step),
        out_shape=[square] * 2,
        in_specs=[in_vmem] * columns,
        out_specs=[in_vmem] * 2,
        cost_estimate=pl.CostEstimate(flops=flops, bytes_accessed=columns * span * slab * 4, transcendentals=0),
        name="near",
    )(*near)
    mixed = jax.ShapeDtypeStruct((slab, full), bf16)
    *late, mixed_rows, mixed_cols = pl.pallas_call(
        functools.partial(far_kernel, hosts, per_host, tuple(order), slab, aux, step),
        out_shape=[piece] * (hosts - cut) + [mixed] * 2,
        in_specs=[in_smem] * 3 + [in_vmem] * (3 + columns),
        out_specs=[in_vmem] * (hosts - cut + 2),
        scratch_shapes=[pltpu.VMEM((slab, full), f32)] * 2
        + [pltpu.VMEM((span, full), bf16)] * 2
        + plan_scratch,
        name="far",
    )(table, ids, occ_energy, virt_energy.reshape(1, full), one, two, *far)
    early = pl.pallas_call(
        functools.partial(rest_kernel, columns, slab, aux),
        out_shape=[piece] * cut,
        in_specs=[in_vmem] * (2 + columns),
        out_specs=[in_vmem] * cut,
        cost_estimate=pl.CostEstimate(flops=flops, bytes_accessed=columns * span * slab * 4, transcendentals=0),
        name="rest",
    )(mixed_rows, mixed_cols, *near)

    home = {}
    for s in reversed(range(cut, hosts)):
        home[s] = over_occ(late[s - cut], s)
    for s in reversed(range(1, cut)):
        home[s] = over_occ(early[s], s)
    home[0] = early[0]

    strips = next(c for c in (4, 3, 2, 1) if aux % (c * STRIP) == 0)
    block = strips * STRIP
    return pl.pallas_call(
        functools.partial(scatter_kernel, hosts, per_host, orbitals, strips),
        grid=(aux // block,),
        out_shape=jax.ShapeDtypeStruct((slab, local), f32),
        in_specs=[in_smem, in_smem] + [pl.BlockSpec((block, 2 * slab), lambda g: (g, 0))] * hosts,
        out_specs=pl.BlockSpec((slab, block * orbitals), lambda g: (0, g)),
        scratch_shapes=[pltpu.VMEM((2 * hosts * STRIP, STRIP * orbitals), bf16)] + plan_scratch,
        name="scatter",
    )(table, ids, *[home[s] for s in range(hosts)])


def plain_body(hosts, columns, factors, occ_energy, virt_energy, pair_table, pair_count):
    per_host = pair_table.shape[0]
    tables = lax.all_gather(pair_table, "occ", axis=0, tiled=True)
    counts = lax.all_gather(pair_count, "occ", axis=0, tiled=True)
    entries = jnp.arange(hosts * per_host, dtype=jnp.int32)
    active = entries % per_host < jnp.repeat(counts, per_host)
    slot_count = -(-(per_host * hosts // 2) // hosts)
    ranking = jnp.cumsum(active.astype(jnp.int32)) - 1
    targets = jnp.arange(hosts * slot_count, dtype=jnp.int32)
    select = (active[None, :] & (ranking[None, :] == targets[:, None])).astype(jnp.int32)
    plan = jnp.sum(select[:, :, None] * tables[None, :, :], axis=1).reshape(hosts, slot_count, 2)
    enabled = jnp.max(select, axis=1).reshape(hosts, slot_count)
    column = lax.axis_index("virt")
    myself = lax.axis_index("occ")
    orbitals = occ_energy.shape[0]
    slab = factors.shape[0]
    aux = factors.shape[1] // orbitals
    own = lax.dynamic_slice_in_dim(virt_energy, column * slab, slab)
    cube = factors.reshape(slab, aux, orbitals)
    gamma = jnp.zeros((slab, aux, orbitals), jnp.float32)
    for position in range(slot_count):
        wanted = plan[:, position].T.reshape(-1)
        onehot = (wanted[:, None] == jnp.arange(orbitals, dtype=jnp.int32)[None, :]).astype(jnp.bfloat16)
        picked = lax.dot_general(
            cube, onehot, (((2,), (1,)), ((), ())), preferred_element_type=jnp.float32
        ).astype(jnp.bfloat16)
        outgoing = picked.reshape(slab, aux, 2, hosts)
        both = lax.all_to_all(outgoing, "occ", split_axis=3, concat_axis=1, tiled=True)
        both = lax.all_gather(both, "virt", axis=0, tiled=True)
        left, right = both[:, :, 0, 0], both[:, :, 1, 0]
        mine = lax.dynamic_index_in_dim(plan[:, position], myself, 0, keepdims=False)
        live = lax.dynamic_index_in_dim(enabled[:, position], myself, 0, keepdims=False).astype(jnp.float32)
        left_slab = lax.dynamic_slice_in_dim(left, column * slab, slab, 0)
        right_slab = lax.dynamic_slice_in_dim(right, column * slab, slab, 0)
        dims = (((1,), (1,)), ((), ()))
        rows = lax.dot_general(left_slab, right, dims, preferred_element_type=jnp.float32)
        cols = lax.dot_general(right_slab, left, dims, preferred_element_type=jnp.float32)
        energy = jnp.take(occ_energy, mine[0]) + jnp.take(occ_energy, mine[1])
        den = energy - own[:, None] - virt_energy[None, :]
        mixed_rows = ((2.0 * rows - cols) / den * live).astype(jnp.bfloat16)
        mixed_cols = ((2.0 * cols - rows) / den * live).astype(jnp.bfloat16)
        toward_first = jnp.dot(mixed_rows, right, preferred_element_type=jnp.float32)
        toward_second = jnp.dot(mixed_cols, left, preferred_element_type=jnp.float32)
        packed = jnp.stack([toward_first.astype(jnp.bfloat16), toward_second.astype(jnp.bfloat16)], axis=2)
        packed = packed.reshape(slab, hosts, aux, 2, 1)
        back = lax.all_to_all(packed, "occ", split_axis=1, concat_axis=4, tiled=True)
        gamma = gamma + lax.dot_general(
            back.reshape(slab, aux, 2 * hosts), onehot, (((2,), (0,)), ((), ())), preferred_element_type=jnp.float32
        )
    return gamma.reshape(factors.shape)


def solution(mesh):
    hosts, columns = mesh.shape["occ"], mesh.shape["virt"]

    def body(factors, occ_energy, virt_energy, pair_table, pair_count):
        slab, local = factors.shape
        orbitals = occ_energy.shape[0]
        fits = (
            hosts <= 8
            and hosts & (hosts - 1) == 0
            and columns & (columns - 1) == 0
            and pair_table.shape[0] == 2
            and (local // orbitals) % STRIP == 0
            and (STRIP * orbitals) % LANES == 0
            and (2 * slab) % LANES == 0
        )
        run = fast_body if fits else plain_body
        return run(hosts, columns, factors, occ_energy, virt_energy, pair_table, pair_count)

    in_specs = (P("virt", "occ"), P(), P(), P("occ", None), P("occ"))
    return jax.shard_map(body, mesh=mesh, in_specs=in_specs, out_specs=P("virt", "occ"), check_vma=False)
```

time: 128 us -> 113 us (0.88)
  waiting for transfers between devices: 70.4 us -> 56 us
  Pallas kernels: 22.7 us -> 20.2 us
  starting transfers between devices: 26.3 us -> 28.7 us
  local copies, waits for them, and re-layouts: 4.91 us -> 6.9 us
  other arithmetic: 2.22 us -> 0.38 us
    ppermute x17 -> x20, waiting for transfers between devices: 62.9 us -> 48.6 us  [the longest x14 38.4 us: over_occ(): return lax.ppermute(x, 'occ', [(d, d ^ s) for d in range(hosts)])]
    pallas_call x1, Pallas kernels: 6.67 us -> 2.46 us  [fast_body(): pl.pallas_call(functools.partial(select_kernel, hosts, per_host, orbitals...]
    pallas_call x1 -> x3, Pallas kernels: 8.93 us -> 11.8 us  [the longest x1 4.89 us: fast_body(): pl.pallas_call(functools.partial(far_kernel, hosts, per_host, tuple(order...]
    ppermute x17 -> x20, starting transfers between devices: 22.2 us -> 24.5 us  [the longest x14 20.8 us: over_occ(): return lax.ppermute(x, 'occ', [(d, d ^ s) for d in range(hosts)])]
    unnamed x29 -> x38, local copies, waits for them, and re-layouts: 2.63 us -> 4.79 us
    concatenate x1 -> x0, other arithmetic: 1.33 us -> none  [fast_body(): jnp.concatenate([lax.dynamic_slice_in_dim(energies, column ^ o, 1, 0) for...]
  transfers between devices with their start and end apart: 20 -> 23, of which waited for: 16 -> 15; matrix products, arithmetic and copies ran while one was open for 3% -> 1% of each run, Pallas kernels for 0% -> 3%
where the time goes in v2:
time: 113 us
  waiting for transfers between devices  56 us (50%)
  starting transfers between devices  28.7 us (25%)
  Pallas kernels  20.2 us (18%)
  local copies, waits for them, and re-layouts  6.9 us (6%)
    ppermute x14, waiting for transfers between devices, over_occ(): return lax.ppermute(x, 'occ', [(d, d ^ s) for d in range(hosts)])  38.4 us
    ppermute x14, starting transfers between devices, over_occ(): return lax.ppermute(x, 'occ', [(d, d ^ s) for d in range(hosts)])  20.8 us
    ppermute x6, waiting for transfers between devices, over_virt(): return lax.ppermute(x, 'virt', [(d, d ^ s) for d in range(columns)])  10.2 us
    ppermute x3, waiting for transfers between devices, fast_body(): other = lax.ppermute(table, 'occ', [(d, d ^ shift) for d in range(hosts)])  7.43 us
    pallas_call x1, Pallas kernels, fast_body(): pl.pallas_call(functools.partial(scatter_kernel, hosts, per_host, orbital...  5.91 us
    pallas_call x1, Pallas kernels, fast_body(): pl.pallas_call(functools.partial(far_kernel, hosts, per_host, tuple(order...  4.89 us
    unnamed x38, local copies, waits for them, and re-layouts  4.79 us
    ppermute x3, starting transfers between devices, fast_body(): other = lax.ppermute(table, 'occ', [(d, d ^ shift) for d in range(hosts)])  4.12 us
  transfers between devices with their start and end apart: 23, of which 15 were waited for; matrix products, arithmetic and copies ran while one was open for 1% of the time, Pallas kernels for 3%

profile of v2, /device:TPU:8, one launch (start us, length us, event | category | flops | bytes accessed | tf_op | source)
XLA Modules:
  0.0 113.0 jit_solution(8095098526536404013)
XLA Ops:
  1.5 1.5 %collective-permute-start = (s32[1,5]{1,0:T(1,128)S(1)}, s32[1,5]{1,0:T(1,128)S(1)}, u32[]{:S(2)}, u32[]{:S(2)}) collective-permute-start(s32[1,5]{1,0:T(1,128)S(1)} %pad_add_fusion.3), channel_id=1, source_target_pairs={{0,4},{4,0},{8,12},{12,8},{16,20},{20,16},{24,28},{28,24},{1,5},{5... | collective-permute-start | bytes 68 | tf_op jit(solution)/shard_map/ppermute | solution.py:176
  3.0 2.0 %collective-permute-done = s32[1,5]{1,0:T(1,128)S(1)} collective-permute-done((s32[1,5]{1,0:T(1,128)S(1)}, s32[1,5]{1,0:T(1,128)S(1)}, u32[]{:S(2)}, u32[]{:S(2)}) %collective-permute-start) | collective-permute-done | bytes 52 | tf_op jit(solution)/shard_map/ppermute | solution.py:176
  5.1 3.6 %collective-permute-done.1 = s32[2,5]{1,0:T(2,128)S(1)} collective-permute-done((s32[2,5]{1,0:T(2,128)S(1)}, s32[2,5]{1,0:T(2,128)S(1)}, u32[]{:S(2)}, u32[]{:S(2)}) %collective-permute-start.1) | collective-permute-done | bytes 72 | tf_op jit(solution)/shard_map/ppermute | solution.py:176
  8.8 2.6 %collective-permute-start.2 = (s32[4,5]{1,0:T(4,128)S(1)}, s32[4,5]{1,0:T(4,128)S(1)}, u32[]{:S(2)}, u32[]{:S(2)}) collective-permute-start(s32[4,5]{1,0:T(4,128)S(1)} %pad_add_fusion.1), channel_id=1, source_target_pairs={{0,16},{4,20},{8,24},{12,28},{16,0},{20,4},{24,8},{28,12},{1,17},{... | collective-permute-start | bytes 248 | tf_op jit(solution)/shard_map/ppermute | solution.py:176
  11.5 1.8 %collective-permute-done.2 = s32[4,5]{1,0:T(4,128)S(1)} collective-permute-done((s32[4,5]{1,0:T(4,128)S(1)}, s32[4,5]{1,0:T(4,128)S(1)}, u32[]{:S(2)}, u32[]{:S(2)}) %collective-permute-start.2) | collective-permute-done | bytes 112 | tf_op jit(solution)/shard_map/ppermute | solution.py:176
  13.4 2.3 %copy-done = bf16[192,12288]{1,0:T(8,128)(2,1)S(1)} copy-done((bf16[192,12288]{1,0:T(8,128)(2,1)S(1)}, bf16[192,12288]{1,0:T(8,128)(2,1)}, u32[]{:S(2)}) %copy-start) | copy-done | bytes 4718616
  15.7 2.5 %select.1 = (bf16[192,384]{1,0:T(8,128)(2,1)S(1)}, bf16[192,384]{1,0:T(8,128)(2,1)S(1)}, bf16[192,384]{1,0:T(8,128)(2,1)S(1)}, bf16[192,384]{1,0:T(8,128)(2,1)S(...) custom-call(s32[8,5]{1,0:T(8,128)S(1)} %pad_add_fusion.tab_ref, ...), custom_call_target="tpu_custom_call" | custom-call | tf_op jit(solution)/shard_map/select/pallas_call | solution.py:188
  18.2 1.6 %collective-permute-start.3 = (bf16[192,384]{1,0:T(8,128)(2,1)S(1)}, bf16[192,384]{1,0:T(8,128)(2,1)S(1)}, u32[]{:S(2)}, u32[]{:S(2)}) collective-permute-start(bf16[192,384]{1,0:T(8,128)(2,1)S(1)} %get-tuple-element.26), channel_id=1, source_target_pairs={{0,4},{4,0},{8,12},{12,8},{16,20},{20,16},{24,28},{28,24},{1,5},{5... | collective-permute-start | bytes 442376 | tf_op jit(solution)/shard_map/ppermute | solution.py:199
  21.7 2.6 %collective-permute-start.9 = (bf16[192,384]{1,0:T(8,128)(2,1)S(1)}, bf16[192,384]{1,0:T(8,128)(2,1)S(1)}, u32[]{:S(2)}, u32[]{:S(2)}) collective-permute-start(bf16[192,384]{1,0:T(8,128)(2,1)S(1)} %get-tuple-element.31), channel_id=1, source_target_pairs={{0,16},{4,20},{8,24},{12,28},{16,0},{20,4},{24,8},{28,12},{1,17},{... | collective-permute-start | bytes 442376 | tf_op jit(solution)/shard_map/ppermute | solution.py:199
  25.6 1.6 %collective-permute-start.11 = (bf16[192,384]{1,0:T(8,128)(2,1)S(1)}, bf16[192,384]{1,0:T(8,128)(2,1)S(1)}, u32[]{:S(2)}, u32[]{:S(2)}) collective-permute-start(bf16[192,384]{1,0:T(8,128)(2,1)S(1)} %get-tuple-element.33), channel_id=1, source_target_pairs={{0,24},{4,28},{8,16},{12,20},{16,8},{20,12},{24,0},{28,4},{1,25},{... | collective-permute-start | bytes 442376 | tf_op jit(solution)/shard_map/ppermute | solution.py:199
  28.0 1.5 %collective-permute-done.5 = bf16[192,384]{1,0:T(8,128)(2,1)S(1)} collective-permute-done((bf16[192,384]{1,0:T(8,128)(2,1)S(1)}, bf16[192,384]{1,0:T(8,128)(2,1)S(1)}, u32[]{:S(2)}, u32[]{:S(2)}) %collective-permute-start.5) | collective-permute-done | bytes 147488 | tf_op jit(solution)/shard_map/ppermute | solution.py:199
  29.6 1.6 %collective-permute-start.6 = (bf16[768,384]{1,0:T(8,128)(2,1)S(1)}, bf16[768,384]{1,0:T(8,128)(2,1)S(1)}, u32[]{:S(2)}, u32[]{:S(2)}) collective-permute-start(bf16[768,384]{1,0:T(8,128)(2,1)S(1)} %constant_dynamic-update-slice_fusion.rest_0_), channel_id=1, source_target_pairs={{0,2},{1,3},{2,0},{3,1},{4,6},{5,7},{6,4},{7,5},{8,10},{9,11},{10,... | collective-permute-start | bytes 1769480 | tf_op jit(solution)/shard_map/ppermute | solution.py:202
  31.2 6.8 %collective-permute-done.9 = bf16[192,384]{1,0:T(8,128)(2,1)S(1)} collective-permute-done((bf16[192,384]{1,0:T(8,128)(2,1)S(1)}, bf16[192,384]{1,0:T(8,128)(2,1)S(1)}, u32[]{:S(2)}, u32[]{:S(2)}) %collective-permute-start.9) | collective-permute-done | bytes 147488 | tf_op jit(solution)/shard_map/ppermute | solution.py:199
  38.0 3.1 %collective-permute-done.10 = bf16[192,384]{1,0:T(8,128)(2,1)S(1)} collective-permute-done((bf16[192,384]{1,0:T(8,128)(2,1)S(1)}, bf16[192,384]{1,0:T(8,128)(2,1)S(1)}, u32[]{:S(2)}, u32[]{:S(2)}) %collective-permute-start.10) | collective-permute-done | bytes 147488 | tf_op jit(solution)/shard_map/ppermute | solution.py:199
  41.2 3.5 %collective-permute-done.11 = bf16[192,384]{1,0:T(8,128)(2,1)S(1)} collective-permute-done((bf16[192,384]{1,0:T(8,128)(2,1)S(1)}, bf16[192,384]{1,0:T(8,128)(2,1)S(1)}, u32[]{:S(2)}, u32[]{:S(2)}) %collective-permute-start.11) | collective-permute-done | bytes 147488 | tf_op jit(solution)/shard_map/ppermute | solution.py:199
  44.8 1.9 %collective-permute-done.12 = bf16[192,384]{1,0:T(8,128)(2,1)S(1)} collective-permute-done((bf16[192,384]{1,0:T(8,128)(2,1)S(1)}, bf16[192,384]{1,0:T(8,128)(2,1)S(1)}, u32[]{:S(2)}, u32[]{:S(2)}) %collective-permute-start.12) | collective-permute-done | bytes 147488 | tf_op jit(solution)/shard_map/ppermute | solution.py:199
  46.7 1.5 %collective-permute-start.13 = (bf16[768,384]{1,0:T(8,128)(2,1)S(1)}, bf16[768,384]{1,0:T(8,128)(2,1)S(1)}, u32[]{:S(2)}, u32[]{:S(2)}) collective-permute-start(bf16[768,384]{1,0:T(8,128)(2,1)S(1)} %constant_dynamic-update-slice_fusion.4.rest_0_), channel_id=1, source_target_pairs={{0,2},{1,3},{2,0},{3,1},{4,6},{5,7},{6,4},{7,5},{8,10},{9,11},{10,... | collective-permute-start | bytes 1769480 | tf_op jit(solution)/shard_map/ppermute | solution.py:202
  48.8 10.1 %collective-permute-done.13.rest_1_ = bf16[768,384]{1,0:T(8,128)(2,1)S(1)} collective-permute-done((bf16[768,384]{1,0:T(8,128)(2,1)S(1)}, bf16[768,384]{1,0:T(8,128)(2,1)S(1)}, u32[]{:S(2)}, u32[]{:S(2)}) %collective-permute-start.13) | collective-permute-done | bytes 589856 | tf_op jit(solution)/shard_map/ppermute | solution.py:202
  62.0 3.6 %near.1 = (f32[192,768]{1,0:T(8,128)}, f32[192,768]{1,0:T(8,128)}) custom-call(bf16[768,384]{1,0:T(8,128)(2,1)} %copy-done.3, bf16[768,384]{1,0:T(8,128)(2,1)} %copy-done.4, bf16[768,384]{1,0:T(8,128)(2,1)} %copy-done.5, bf16[768,384]{1,0:T(8,128)(2,1)} %copy-done.6), custom_call_target="tpu_custom_call" | custom-call | flops 452984832 | bytes 2359296 | tf_op jit(solution)/shard_map/near/pallas_call | solution.py:224
  65.6 4.9 %far.1 = (bf16[192,384]{1,0:T(8,128)(2,1)}, bf16[192,384]{1,0:T(8,128)(2,1)}, bf16[192,384]{1,0:T(8,128)(2,1)}, bf16[192,384]{1,0:T(8,128)(2,1)}, bf16[192,768]{1,0:T(8,128)(2,1)}, /*index=5*/bf16[192,768]{1,0:T(8,128)(2,1)}) custom-call(s32[8,5]{1,0:T(8,128)} %copy-done.1, s32[2]{0:T(128)} %copy-done.2, f32[64]{0:T(128)} %occ_ref.1, ...), custom_call_target="tpu_custom_call" | custom-call | tf_op jit(solution)/shard_map/far/pallas_call | solution.py:233
  70.5 3.3 %rest.1 = (bf16[192,384]{1,0:T(8,128)(2,1)}, bf16[192,384]{1,0:T(8,128)(2,1)}, bf16[192,384]{1,0:T(8,128)(2,1)}, bf16[192,384]{1,0:T(8,128)(2,1)}) custom-call(bf16[192,768]{1,0:T(8,128)(2,1)} %get-tuple-element.35.rows_ref, bf16[192,768]{1,0:T(8,128)(2,1)} %get-tuple-element.36.cols_ref, bf16[768,384]{1,0:T(8,128)(2,1)} %copy-done.3, ...), custom_call_target="tpu_custom_call" | custom-call | flops 452984832 | bytes 2359296 | tf_op jit(solution)/shard_map/rest/pallas_call | solution.py:243
  73.8 2.1 %collective-permute-start.16 = (bf16[192,384]{1,0:T(8,128)(2,1)}, bf16[192,384]{1,0:T(8,128)(2,1)S(1)}, u32[]{:S(2)}, u32[]{:S(2)}) collective-permute-start(bf16[192,384]{1,0:T(8,128)(2,1)} %get-tuple-element.38), channel_id=1, source_target_pairs={{0,4},{4,0},{8,12},{12,8},{16,20},{20,16},{24,28},{28,24},{1,5},{5... | collective-permute-start | bytes 442376 | tf_op jit(solution)/shard_map/ppermute | solution.py:199
  77.4 2.1 %collective-permute-start.19 = (bf16[192,384]{1,0:T(8,128)(2,1)}, bf16[192,384]{1,0:T(8,128)(2,1)S(1)}, u32[]{:S(2)}, u32[]{:S(2)}) collective-permute-start(bf16[192,384]{1,0:T(8,128)(2,1)} %get-tuple-element.41), channel_id=1, source_target_pairs={{0,16},{4,20},{8,24},{12,28},{16,0},{20,4},{24,8},{28,12},{1,17},{... | collective-permute-start | bytes 442376 | tf_op jit(solution)/shard_map/ppermute | solution.py:199
  79.5 2.3 %collective-permute-start.20 = (bf16[192,384]{1,0:T(8,128)(2,1)}, bf16[192,384]{1,0:T(8,128)(2,1)S(1)}, u32[]{:S(2)}, u32[]{:S(2)}) collective-permute-start(bf16[192,384]{1,0:T(8,128)(2,1)} %get-tuple-element.42), channel_id=1, source_target_pairs={{0,20},{4,16},{8,28},{12,24},{16,4},{20,0},{24,12},{28,8},{1,21},{... | collective-permute-start | bytes 442376 | tf_op jit(solution)/shard_map/ppermute | solution.py:199
  83.0 1.8 %collective-permute-done.17.rest_2_ = bf16[192,384]{1,0:T(8,128)(2,1)S(1)} collective-permute-done((bf16[192,384]{1,0:T(8,128)(2,1)}, bf16[192,384]{1,0:T(8,128)(2,1)S(1)}, u32[]{:S(2)}, u32[]{:S(2)}) %collective-permute-start.17) | collective-permute-done | bytes 147488 | tf_op jit(solution)/shard_map/ppermute | solution.py:199
  84.8 1.9 %collective-permute-start.22 = (bf16[192,384]{1,0:T(8,128)(2,1)}, bf16[192,384]{1,0:T(8,128)(2,1)S(1)}, u32[]{:S(2)}, u32[]{:S(2)}) collective-permute-start(bf16[192,384]{1,0:T(8,128)(2,1)} %get-tuple-element.44), channel_id=1, source_target_pairs={{0,28},{4,24},{8,20},{12,16},{16,12},{20,8},{24,4},{28,0},{1,29},{... | collective-permute-start | bytes 442376 | tf_op jit(solution)/shard_map/ppermute | solution.py:199
  86.8 1.5 %collective-permute-done.18.rest_3_ = bf16[192,384]{1,0:T(8,128)(2,1)S(1)} collective-permute-done((bf16[192,384]{1,0:T(8,128)(2,1)}, bf16[192,384]{1,0:T(8,128)(2,1)S(1)}, u32[]{:S(2)}, u32[]{:S(2)}) %collective-permute-start.18) | collective-permute-done | bytes 147488 | tf_op jit(solution)/shard_map/ppermute | solution.py:199
  88.3 1.5 %collective-permute-done.19.rest_4_ = bf16[192,384]{1,0:T(8,128)(2,1)S(1)} collective-permute-done((bf16[192,384]{1,0:T(8,128)(2,1)}, bf16[192,384]{1,0:T(8,128)(2,1)S(1)}, u32[]{:S(2)}, u32[]{:S(2)}) %collective-permute-start.19) | collective-permute-done | bytes 147488 | tf_op jit(solution)/shard_map/ppermute | solution.py:199
  89.8 10.0 %collective-permute-done.20.rest_5_ = bf16[192,384]{1,0:T(8,128)(2,1)S(1)} collective-permute-done((bf16[192,384]{1,0:T(8,128)(2,1)}, bf16[192,384]{1,0:T(8,128)(2,1)S(1)}, u32[]{:S(2)}, u32[]{:S(2)}) %collective-permute-start.20) | collective-permute-done | bytes 147488 | tf_op jit(solution)/shard_map/ppermute | solution.py:199
  99.9 4.0 %collective-permute-done.21.rest_6_ = bf16[192,384]{1,0:T(8,128)(2,1)S(1)} collective-permute-done((bf16[192,384]{1,0:T(8,128)(2,1)}, bf16[192,384]{1,0:T(8,128)(2,1)S(1)}, u32[]{:S(2)}, u32[]{:S(2)}) %collective-permute-start.21) | collective-permute-done | bytes 147488 | tf_op jit(solution)/shard_map/ppermute | solution.py:199
  103.9 2.5 %collective-permute-done.22.rest_7_ = bf16[192,384]{1,0:T(8,128)(2,1)S(1)} collective-permute-done((bf16[192,384]{1,0:T(8,128)(2,1)}, bf16[192,384]{1,0:T(8,128)(2,1)S(1)}, u32[]{:S(2)}, u32[]{:S(2)}) %collective-permute-start.22) | collective-permute-done | bytes 147488 | tf_op jit(solution)/shard_map/ppermute | solution.py:199
  107.0 5.9 %scatter.1 = f32[192,12288]{1,0:T(8,128)} custom-call(s32[8,5]{1,0:T(8,128)} %copy-done.1, s32[2]{0:T(128)} %copy-done.2, bf16[192,384]{1,0:T(8,128)(2,1)} %get-tuple-element.37.rest_0_, bf16[192,384]{1,0:T(8,128)(2,1)} %copy-done.9, bf16[192,384]{1,0:T(8,128)(2,1)} %copy-done.10, bf16[192,384]{1,0:T(8,128)(2,1)} %copy-done.11, bf16[192,384]{1,0:T(8,128)(2,1)} %copy-done.12, ...), custom_call_target="tpu_custom_call" | custom-call | tf_op jit(solution)/shard_map/scatter/pallas_call | solution.py:261
  (66 shorter events, 12.2 us)
Async XLA Ops:
  1.5 3.6 %collective-permute-start = (s32[1,5]{1,0:T(1,128)S(1)}, s32[1,5]{1,0:T(1,128)S(1)}, u32[]{:S(2)}, u32[]{:S(2)}) collective-permute-start(s32[1,5]{1,0:T(1,128)S(1)} %pad_add_fusion.3), channel_id=1, source_target_pairs={{0,4},{4,0},{8,12},{12,8},{16,20},{20,16},{24,28},{28,24},{1,5},{5... | collective-permute-start | bytes 68 | tf_op jit(solution)/shard_map/ppermute | solution.py:176
  5.1 3.6 %collective-permute-start.1 = (s32[2,5]{1,0:T(2,128)S(1)}, s32[2,5]{1,0:T(2,128)S(1)}, u32[]{:S(2)}, u32[]{:S(2)}) collective-permute-start(s32[2,5]{1,0:T(2,128)S(1)} %pad_add_fusion.2), channel_id=1, source_target_pairs={{0,8},{4,12},{8,0},{12,4},{16,24},{20,28},{24,16},{28,20},{1,9},{5... | collective-permute-start | bytes 128 | tf_op jit(solution)/shard_map/ppermute | solution.py:176
  8.8 4.5 %collective-permute-start.2 = (s32[4,5]{1,0:T(4,128)S(1)}, s32[4,5]{1,0:T(4,128)S(1)}, u32[]{:S(2)}, u32[]{:S(2)}) collective-permute-start(s32[4,5]{1,0:T(4,128)S(1)} %pad_add_fusion.1), channel_id=1, source_target_pairs={{0,16},{4,20},{8,24},{12,28},{16,0},{20,4},{24,8},{28,12},{1,17},{... | collective-permute-start | bytes 248 | tf_op jit(solution)/shard_map/ppermute | solution.py:176
  11.5 54.1 %copy-start.2 = (s32[2]{0:T(128)}, s32[2]{0:T(128)S(1)}, u32[]{:S(2)}) copy-start(s32[2]{0:T(128)S(1)} %pad_add_fusion.4.ids_ref) | copy-start | bytes 28
  15.7 49.9 %copy-start.1 = (s32[8,5]{1,0:T(8,128)}, s32[8,5]{1,0:T(8,128)S(1)}, u32[]{:S(2)}) copy-start(s32[8,5]{1,0:T(8,128)S(1)} %pad_add_fusion.tab_ref) | copy-start | bytes 484
  18.2 7.5 %collective-permute-start.3 = (bf16[192,384]{1,0:T(8,128)(2,1)S(1)}, bf16[192,384]{1,0:T(8,128)(2,1)S(1)}, u32[]{:S(2)}, u32[]{:S(2)}) collective-permute-start(bf16[192,384]{1,0:T(8,128)(2,1)S(1)} %get-tuple-element.26), channel_id=1, source_target_pairs={{0,4},{4,0},{8,12},{12,8},{16,20},{20,16},{24,28},{28,24},{1,5},{5... | collective-permute-start | bytes 442376 | tf_op jit(solution)/shard_map/ppermute | solution.py:199
  19.7 7.6 %collective-permute-start.4 = (bf16[192,384]{1,0:T(8,128)(2,1)S(1)}, bf16[192,384]{1,0:T(8,128)(2,1)S(1)}, u32[]{:S(2)}, u32[]{:S(2)}) collective-permute-start(bf16[192,384]{1,0:T(8,128)(2,1)S(1)} %get-tuple-element.27), channel_id=1, source_target_pairs={{0,8},{4,12},{8,0},{12,4},{16,24},{20,28},{24,16},{28,20},{1,9},{5... | collective-permute-start | bytes 442376 | tf_op jit(solution)/shard_map/ppermute | solution.py:199
  20.2 9.4 %collective-permute-start.5 = (bf16[192,384]{1,0:T(8,128)(2,1)S(1)}, bf16[192,384]{1,0:T(8,128)(2,1)S(1)}, u32[]{:S(2)}, u32[]{:S(2)}) collective-permute-start(bf16[192,384]{1,0:T(8,128)(2,1)S(1)} %get-tuple-element.28), channel_id=1, source_target_pairs={{0,12},{4,8},{8,4},{12,0},{16,28},{20,24},{24,20},{28,16},{1,13},{... | collective-permute-start | bytes 442376 | tf_op jit(solution)/shard_map/ppermute | solution.py:199
  21.7 16.3 %collective-permute-start.9 = (bf16[192,384]{1,0:T(8,128)(2,1)S(1)}, bf16[192,384]{1,0:T(8,128)(2,1)S(1)}, u32[]{:S(2)}, u32[]{:S(2)}) collective-permute-start(bf16[192,384]{1,0:T(8,128)(2,1)S(1)} %get-tuple-element.31), channel_id=1, source_target_pairs={{0,16},{4,20},{8,24},{12,28},{16,0},{20,4},{24,8},{28,12},{1,17},{... | collective-permute-start | bytes 442376 | tf_op jit(solution)/shard_map/ppermute | solution.py:199
  24.3 16.9 %collective-permute-start.10 = (bf16[192,384]{1,0:T(8,128)(2,1)S(1)}, bf16[192,384]{1,0:T(8,128)(2,1)S(1)}, u32[]{:S(2)}, u32[]{:S(2)}) collective-permute-start(bf16[192,384]{1,0:T(8,128)(2,1)S(1)} %get-tuple-element.32), channel_id=1, source_target_pairs={{0,20},{4,16},{8,28},{12,24},{16,4},{20,0},{24,12},{28,8},{1,21},{... | collective-permute-start | bytes 442376 | tf_op jit(solution)/shard_map/ppermute | solution.py:199
  25.6 19.1 %collective-permute-start.11 = (bf16[192,384]{1,0:T(8,128)(2,1)S(1)}, bf16[192,384]{1,0:T(8,128)(2,1)S(1)}, u32[]{:S(2)}, u32[]{:S(2)}) collective-permute-start(bf16[192,384]{1,0:T(8,128)(2,1)S(1)} %get-tuple-element.33), channel_id=1, source_target_pairs={{0,24},{4,28},{8,16},{12,20},{16,8},{20,12},{24,0},{28,4},{1,25},{... | collective-permute-start | bytes 442376 | tf_op jit(solution)/shard_map/ppermute | solution.py:199
  27.3 19.4 %collective-permute-start.12 = (bf16[192,384]{1,0:T(8,128)(2,1)S(1)}, bf16[192,384]{1,0:T(8,128)(2,1)S(1)}, u32[]{:S(2)}, u32[]{:S(2)}) collective-permute-start(bf16[192,384]{1,0:T(8,128)(2,1)S(1)} %get-tuple-element.34), channel_id=1, source_target_pairs={{0,28},{4,24},{8,20},{12,16},{16,12},{20,8},{24,4},{28,0},{1,29},{... | collective-permute-start | bytes 442376 | tf_op jit(solution)/shard_map/ppermute | solution.py:199
  29.6 30.7 %copy-start.3 = (bf16[768,384]{1,0:T(8,128)(2,1)}, bf16[768,384]{1,0:T(8,128)(2,1)S(1)}, u32[]{:S(2)}) copy-start(bf16[768,384]{1,0:T(8,128)(2,1)S(1)} %constant_dynamic-update-slice_fusion.rest_0_) | copy-start | bytes 1769476
  29.6 18.6 %collective-permute-start.6 = (bf16[768,384]{1,0:T(8,128)(2,1)S(1)}, bf16[768,384]{1,0:T(8,128)(2,1)S(1)}, u32[]{:S(2)}, u32[]{:S(2)}) collective-permute-start(bf16[768,384]{1,0:T(8,128)(2,1)S(1)} %constant_dynamic-update-slice_fusion.rest_0_), channel_id=1, source_target_pairs={{0,2},{1,3},{2,0},{3,1},{4,6},{5,7},{6,4},{7,5},{8,10},{9,11},{10,... | collective-permute-start | bytes 1769480 | tf_op jit(solution)/shard_map/ppermute | solution.py:202
  46.7 18.9 %copy-start.7 = (bf16[768,384]{1,0:T(8,128)(2,1)}, bf16[768,384]{1,0:T(8,128)(2,1)S(1)}, u32[]{:S(2)}) copy-start(bf16[768,384]{1,0:T(8,128)(2,1)S(1)} %constant_dynamic-update-slice_fusion.4.rest_0_) | copy-start | bytes 1769476
  46.7 12.3 %collective-permute-start.13 = (bf16[768,384]{1,0:T(8,128)(2,1)S(1)}, bf16[768,384]{1,0:T(8,128)(2,1)S(1)}, u32[]{:S(2)}, u32[]{:S(2)}) collective-permute-start(bf16[768,384]{1,0:T(8,128)(2,1)S(1)} %constant_dynamic-update-slice_fusion.4.rest_0_), channel_id=1, source_target_pairs={{0,2},{1,3},{2,0},{3,1},{4,6},{5,7},{6,4},{7,5},{8,10},{9,11},{10,... | collective-permute-start | bytes 1769480 | tf_op jit(solution)/shard_map/ppermute | solution.py:202
  48.2 12.0 %collective-permute-start.7 = (bf16[768,384]{1,0:T(8,128)(2,1)S(1)}, bf16[768,384]{1,0:T(8,128)(2,1)S(1)}, u32[]{:S(2)}, u32[]{:S(2)}) collective-permute-start(bf16[768,384]{1,0:T(8,128)(2,1)S(1)} %constant_dynamic-update-slice_fusion.rest_0_), channel_id=1, source_target_pairs={{0,1},{1,0},{2,3},{3,2},{4,5},{5,4},{6,7},{7,6},{8,9},{9,8},{10,11... | collective-permute-start | bytes 1769480 | tf_op jit(solution)/shard_map/ppermute | solution.py:202
  48.3 12.0 %copy-start.4 = (bf16[768,384]{1,0:T(8,128)(2,1)}, bf16[768,384]{1,0:T(8,128)(2,1)S(1)}, u32[]{:S(2)}) copy-start(bf16[768,384]{1,0:T(8,128)(2,1)S(1)} %collective-permute-done.6.rest_1_) | copy-start | bytes 1769476
  48.3 12.0 %collective-permute-start.8 = (bf16[768,384]{1,0:T(8,128)(2,1)S(1)}, bf16[768,384]{1,0:T(8,128)(2,1)S(1)}, u32[]{:S(2)}, u32[]{:S(2)}) collective-permute-start(bf16[768,384]{1,0:T(8,128)(2,1)S(1)} %collective-permute-done.6.rest_1_), channel_id=1, source_target_pairs={{0,1},{1,0},{2,3},{3,2},{4,5},{5,4},{6,7},{7,6},{8,9},{9,8},{10,11... | collective-permute-start | bytes 1769480 | tf_op jit(solution)/shard_map/ppermute | solution.py:202
  48.8 16.8 %collective-permute-start.14 = (bf16[768,384]{1,0:T(8,128)(2,1)S(1)}, bf16[768,384]{1,0:T(8,128)(2,1)}, u32[]{:S(2)}, u32[]{:S(2)}) collective-permute-start(bf16[768,384]{1,0:T(8,128)(2,1)S(1)} %constant_dynamic-update-slice_fusion.4.rest_0_), channel_id=1, source_target_pairs={{0,1},{1,0},{2,3},{3,2},{4,5},{5,4},{6,7},{7,6},{8,9},{9,8},{10,11... | collective-permute-start | bytes 1769480 | tf_op jit(solution)/shard_map/ppermute | solution.py:202
  59.0 6.6 %collective-permute-start.15 = (bf16[768,384]{1,0:T(8,128)(2,1)S(1)}, bf16[768,384]{1,0:T(8,128)(2,1)}, u32[]{:S(2)}, u32[]{:S(2)}) collective-permute-start(bf16[768,384]{1,0:T(8,128)(2,1)S(1)} %collective-permute-done.13.rest_1_), channel_id=1, source_target_pairs={{0,1},{1,0},{2,3},{3,2},{4,5},{5,4},{6,7},{7,6},{8,9},{9,8},{10,11... | collective-permute-start | bytes 1769480 | tf_op jit(solution)/shard_map/ppermute | solution.py:202
  73.8 8.0 %collective-permute-start.16 = (bf16[192,384]{1,0:T(8,128)(2,1)}, bf16[192,384]{1,0:T(8,128)(2,1)S(1)}, u32[]{:S(2)}, u32[]{:S(2)}) collective-permute-start(bf16[192,384]{1,0:T(8,128)(2,1)} %get-tuple-element.38), channel_id=1, source_target_pairs={{0,4},{4,0},{8,12},{12,8},{16,20},{20,16},{24,28},{28,24},{1,5},{5... | collective-permute-start | bytes 442376 | tf_op jit(solution)/shard_map/ppermute | solution.py:199
  76.0 8.9 %collective-permute-start.17 = (bf16[192,384]{1,0:T(8,128)(2,1)}, bf16[192,384]{1,0:T(8,128)(2,1)S(1)}, u32[]{:S(2)}, u32[]{:S(2)}) collective-permute-start(bf16[192,384]{1,0:T(8,128)(2,1)} %get-tuple-element.39), channel_id=1, source_target_pairs={{0,8},{4,12},{8,0},{12,4},{16,24},{20,28},{24,16},{28,20},{1,9},{5... | collective-permute-start | bytes 442376 | tf_op jit(solution)/shard_map/ppermute | solution.py:199
  76.0 12.3 %collective-permute-start.18 = (bf16[192,384]{1,0:T(8,128)(2,1)}, bf16[192,384]{1,0:T(8,128)(2,1)S(1)}, u32[]{:S(2)}, u32[]{:S(2)}) collective-permute-start(bf16[192,384]{1,0:T(8,128)(2,1)} %get-tuple-element.40), channel_id=1, source_target_pairs={{0,12},{4,8},{8,4},{12,0},{16,28},{20,24},{24,20},{28,16},{1,13},{... | collective-permute-start | bytes 442376 | tf_op jit(solution)/shard_map/ppermute | solution.py:199
  77.4 12.4 %collective-permute-start.19 = (bf16[192,384]{1,0:T(8,128)(2,1)}, bf16[192,384]{1,0:T(8,128)(2,1)S(1)}, u32[]{:S(2)}, u32[]{:S(2)}) collective-permute-start(bf16[192,384]{1,0:T(8,128)(2,1)} %get-tuple-element.41), channel_id=1, source_target_pairs={{0,16},{4,20},{8,24},{12,28},{16,0},{20,4},{24,8},{28,12},{1,17},{... | collective-permute-start | bytes 442376 | tf_op jit(solution)/shard_map/ppermute | solution.py:199
  79.5 20.4 %collective-permute-start.20 = (bf16[192,384]{1,0:T(8,128)(2,1)}, bf16[192,384]{1,0:T(8,128)(2,1)S(1)}, u32[]{:S(2)}, u32[]{:S(2)}) collective-permute-start(bf16[192,384]{1,0:T(8,128)(2,1)} %get-tuple-element.42), channel_id=1, source_target_pairs={{0,20},{4,16},{8,28},{12,24},{16,4},{20,0},{24,12},{28,8},{1,21},{... | collective-permute-start | bytes 442376 | tf_op jit(solution)/shard_map/ppermute | solution.py:199
  81.8 24.6 %copy-start.9 = (bf16[192,384]{1,0:T(8,128)(2,1)}, bf16[192,384]{1,0:T(8,128)(2,1)S(1)}, u32[]{:S(2)}) copy-start(bf16[192,384]{1,0:T(8,128)(2,1)S(1)} %collective-permute-done.16.rest_1_) | copy-start | bytes 442372
  81.8 22.1 %collective-permute-start.21 = (bf16[192,384]{1,0:T(8,128)(2,1)}, bf16[192,384]{1,0:T(8,128)(2,1)S(1)}, u32[]{:S(2)}, u32[]{:S(2)}) collective-permute-start(bf16[192,384]{1,0:T(8,128)(2,1)} %get-tuple-element.43), channel_id=1, source_target_pairs={{0,24},{4,28},{8,16},{12,20},{16,8},{20,12},{24,0},{28,4},{1,25},{... | collective-permute-start | bytes 442376 | tf_op jit(solution)/shard_map/ppermute | solution.py:199
  84.8 21.5 %copy-start.10 = (bf16[192,384]{1,0:T(8,128)(2,1)}, bf16[192,384]{1,0:T(8,128)(2,1)S(1)}, u32[]{:S(2)}) copy-start(bf16[192,384]{1,0:T(8,128)(2,1)S(1)} %collective-permute-done.17.rest_2_) | copy-start | bytes 442372
  84.8 21.5 %collective-permute-start.22 = (bf16[192,384]{1,0:T(8,128)(2,1)}, bf16[192,384]{1,0:T(8,128)(2,1)S(1)}, u32[]{:S(2)}, u32[]{:S(2)}) collective-permute-start(bf16[192,384]{1,0:T(8,128)(2,1)} %get-tuple-element.44), channel_id=1, source_target_pairs={{0,28},{4,24},{8,20},{12,16},{16,12},{20,8},{24,4},{28,0},{1,29},{... | collective-permute-start | bytes 442376 | tf_op jit(solution)/shard_map/ppermute | solution.py:199
  88.3 18.1 %copy-start.11 = (bf16[192,384]{1,0:T(8,128)(2,1)}, bf16[192,384]{1,0:T(8,128)(2,1)S(1)}, u32[]{:S(2)}) copy-start(bf16[192,384]{1,0:T(8,128)(2,1)S(1)} %collective-permute-done.18.rest_3_) | copy-start | bytes 442372
  89.8 16.6 %copy-start.12 = (bf16[192,384]{1,0:T(8,128)(2,1)}, bf16[192,384]{1,0:T(8,128)(2,1)S(1)}, u32[]{:S(2)}) copy-start(bf16[192,384]{1,0:T(8,128)(2,1)S(1)} %collective-permute-done.19.rest_4_) | copy-start | bytes 442372
  (7 other events, 20.4 us)
